TPU v7x, 32 devices: a whole 2x2x4 slice. The times are simulated.
32 devices in a mesh: seq: 4 (over x, core), view: 8 (over z, y).
Axes of the slice: x: 2, y: 2, z: 4, core: 2. Of those that a mesh axis runs over, the one named last changes fastest.
Arguments:
- tokens: bfloat16 [4, 1024, 1024], P('seq', 'view'), may hold values from -6 to 6
- scene_ids: int32 [4, 1024], P('seq', 'view'), may hold values from 0 to 15, as said below
- live_mask: int32 [4, 1024], P('seq', 'view'), may hold values from 0 to 1, as said below
- out_grad: bfloat16 [4, 1024, 1024], P('seq', 'view'), may hold values from -6 to 6
- attention_gain: bfloat16 [1024], replicated, may hold values from 0.5 to 1.5
- input_weight: bfloat16 [1024, 3072], replicated, may hold values from -0.25 to 0.25
- output_weight: bfloat16 [1024, 1024], replicated, may hold values from -1 to 1
- feedforward_gain: bfloat16 [1024], replicated, may hold values from 0.5 to 1.5
- up_weight: bfloat16 [4096, 1024], P(('seq', 'view')), may hold values from -0.1875 to 0.1875
- down_weight: bfloat16 [4096, 1024], P(('seq', 'view')), may hold values from -0.09375 to 0.09375
Outputs:
- layer_out: bfloat16 [4, 1024, 1024], P('seq', 'view')
- tokens_grad: float32 [4, 1024, 1024], P('seq', 'view')
- attention_gain_grad: float32 [1024], replicated
- input_weight_grad: float32 [1024, 3072], replicated
- output_weight_grad: float32 [1024, 1024], replicated
- feedforward_gain_grad: float32 [1024], replicated
- up_weight_grad: float32 [4096, 1024], P(('seq', 'view'))
- down_weight_grad: float32 [4096, 1024], P(('seq', 'view'))
Inputs may be any that keep to these rules, and one draw needn't show every extreme that they name: `scene_ids`: each sequence is made of 64 blocks of 16 consecutive tokens in a drawn order; each block belongs to one scene, each of the sequence's 4 scenes owns 16 blocks, and sequence s holds scenes s * 4 to s * 4 + 3. `live_mask`: constant over each scene; in one sequence every scene is live, in each other sequence exactly one scene is not.
All inputs are finite; a program needn't handle non-finite values.
Results may differ from a plain program's by a relative error of at most 0.015.
Values may be sent and summed in bfloat16 or wider, within the bound.
A program may use at most 256 MiB of HBM per device.

v0:
```python
import math

import jax
import jax.numpy as jnp
from jax import lax
from jax.sharding import PartitionSpec as P

HEADS = 16
HEAD_DIM = 64


EPS = 1e-05
NEGATIVE = -1e30


def layer_norm(values, gain):
    center = values - jnp.mean(values, axis=-1, keepdims=True)
    spread = jnp.mean(center * center, axis=-1, keepdims=True)
    return center * lax.rsqrt(spread + EPS) * gain


def gelu_exact(values):
    return jax.nn.gelu(values, approximate=False)


def plain_dot(left, right):
    return jnp.dot(left, right, preferred_element_type=jnp.float32)


def dot_inner(left, right):
    return lax.dot_general(
        left, right, (((1,), (1,)), ((), ())), preferred_element_type=jnp.float32
    )


def dot_outer(left, right):
    return lax.dot_general(
        left, right, (((0,), (0,)), ((), ())), preferred_element_type=jnp.float32
    )


def split_heads(values):
    return values.reshape(values.shape[0], HEADS, HEAD_DIM)


def masked_scores(queries, keys, query_tags, key_tags, scale):
    raw = jnp.einsum("qhe,khe->hqk", queries, keys, preferred_element_type=jnp.float32) * scale
    allowed = (query_tags[:, None] == key_tags[None, :])[None]
    return (raw, allowed)


def probabilities(queries, keys, query_tags, key_tags, log_total, scale):
    raw, allowed = masked_scores(queries, keys, query_tags, key_tags, scale)
    return jnp.where(
        allowed, jnp.exp(jnp.where(allowed, raw - log_total[:, :, None], NEGATIVE)), 0.0
    )


def in_blocks(step, carry, piece):
    count = piece[0].shape[0]
    size = math.gcd(count, 512)
    number = count // size
    stacked = tuple((member.reshape((number, size) + member.shape[1:]) for member in piece))

    def inner(state, item):
        members, offset = item
        return (step(state, members, offset * size), None)

    result, unused = lax.scan(inner, carry, (stacked, jnp.arange(number, dtype=jnp.int32)))
    return result


def shards(
    tokens,
    scene_ids,
    live_mask,
    out_grad,
    attention_gain,
    input_weight,
    output_weight,
    feedforward_gain,
    up_weight,
    down_weight,
):
    scale = HEAD_DIM ** (-0.5)
    inputs = tokens[0].astype(jnp.float32)
    rows = inputs.shape[0]
    width = inputs.shape[1]
    tags = scene_ids[0] * 2 + live_mask[0]
    live = live_mask[0].astype(jnp.float32)[:, None]
    every_tag = lax.all_gather(tags, "view", axis=0, tiled=True)
    up_full, down_full = (
        lax.all_gather(up_weight, ("seq", "view"), axis=0, tiled=True),
        lax.all_gather(down_weight, ("seq", "view"), axis=0, tiled=True),
    )
    gain_one = attention_gain.astype(jnp.float32)
    gain_two = feedforward_gain.astype(jnp.float32)
    normed = layer_norm(inputs, gain_one).astype(jnp.bfloat16)
    projected = plain_dot(normed, input_weight).astype(jnp.bfloat16)
    query_flat = projected[:, :width]
    queries = split_heads(query_flat)
    keys_own = projected[:, width : 2 * width]
    values_own = projected[:, 2 * width :]

    def attend_step(carry, piece, start):
        peak, total, accum = carry
        key_piece, value_piece = piece
        count = key_piece.shape[0]
        key_tags = lax.dynamic_slice_in_dim(every_tag, start, count)
        raw, allowed = masked_scores(queries, split_heads(key_piece), tags, key_tags, scale)
        masked = jnp.where(allowed, raw, NEGATIVE)
        new_peak = jnp.maximum(peak, jnp.max(masked, axis=-1))
        weights = jnp.where(allowed, jnp.exp(masked - new_peak[:, :, None]), 0.0)
        factor = jnp.exp(peak - new_peak)
        total = total * factor + jnp.sum(weights, axis=-1)
        update = jnp.einsum(
            "hqk,khe->qhe",
            weights.astype(jnp.bfloat16),
            split_heads(value_piece),
            preferred_element_type=jnp.float32,
        )
        accum = accum * jnp.transpose(factor)[:, :, None] + update
        return (new_peak, total, accum)

    start_state = (
        jnp.full((HEADS, rows), NEGATIVE, jnp.float32),
        jnp.zeros((HEADS, rows), jnp.float32),
        jnp.zeros((rows, HEADS, HEAD_DIM), jnp.float32),
    )
    peak, total, accum = in_blocks(
        attend_step,
        start_state,
        (
            lax.all_gather(keys_own, "view", axis=0, tiled=True),
            lax.all_gather(values_own, "view", axis=0, tiled=True),
        ),
    )
    attended_heads = accum / jnp.transpose(total)[:, :, None]
    log_total = peak + jnp.log(total)
    attended_low = attended_heads.reshape(rows, width).astype(jnp.bfloat16)
    branch = plain_dot(attended_low, output_weight)
    middle = inputs + live * branch
    normed_two = layer_norm(middle, gain_two).astype(jnp.bfloat16)
    hidden = dot_inner(normed_two, up_full)
    activated = gelu_exact(hidden).astype(jnp.bfloat16)
    mixed = plain_dot(activated, down_full)
    layer_out = (middle + live * mixed).astype(jnp.bfloat16)[None]
    out_cot = out_grad[0].astype(jnp.float32)
    mixed_cot = (live * out_cot).astype(jnp.bfloat16)
    down_grad = dot_outer(activated, mixed_cot)
    activated_cot = dot_inner(mixed_cot, down_full)
    hidden_cot = jax.vjp(gelu_exact, hidden)[1](activated_cot)[0].astype(jnp.bfloat16)
    up_grad = dot_outer(hidden_cot, normed_two)
    normed_two_cot = plain_dot(hidden_cot, up_full)
    second_pull = jax.vjp(layer_norm, middle, gain_two)[1]
    middle_part, gain_two_grad = second_pull(normed_two_cot)
    middle_cot = out_cot + middle_part
    branch_cot = (live * middle_cot).astype(jnp.bfloat16)
    output_weight_grad = dot_outer(attended_low, branch_cot)
    attended_cot = dot_inner(branch_cot, output_weight).astype(jnp.bfloat16)
    cot_heads = split_heads(attended_cot)
    delta = jnp.transpose(jnp.sum(cot_heads.astype(jnp.float32) * attended_heads, axis=-1))
    seq_len = every_tag.shape[0]

    def back_step(carry, piece, start):
        query_cot, key_value_cot = carry
        key_piece, value_piece = piece
        count = key_piece.shape[0]
        key_tags = lax.dynamic_slice_in_dim(every_tag, start, count)
        key_heads = split_heads(key_piece)
        value_heads = split_heads(value_piece)
        probs = probabilities(queries, key_heads, tags, key_tags, log_total, scale)
        prob_cot = jnp.einsum(
            "qhe,khe->hqk", cot_heads, value_heads, preferred_element_type=jnp.float32
        )
        score_cot = (probs * (prob_cot - delta[:, :, None])).astype(jnp.bfloat16)
        query_cot = (
            query_cot
            + jnp.einsum("hqk,khe->qhe", score_cot, key_heads, preferred_element_type=jnp.float32)
            * scale
        )
        key_cot = (
            jnp.einsum("hqk,qhe->khe", score_cot, queries, preferred_element_type=jnp.float32)
            * scale
        )
        value_cot = jnp.einsum(
            "hqk,qhe->khe",
            probs.astype(jnp.bfloat16),
            cot_heads,
            preferred_element_type=jnp.float32,
        )
        stacked = jnp.concatenate(
            [key_cot.reshape(count, width), value_cot.reshape(count, width)], axis=1
        )
        earlier = lax.dynamic_slice_in_dim(key_value_cot, start, count)
        key_value_cot = lax.dynamic_update_slice_in_dim(key_value_cot, earlier + stacked, start, 0)
        return (query_cot, key_value_cot)

    back_state = (
        jnp.zeros((rows, HEADS, HEAD_DIM), jnp.float32),
        jnp.zeros((seq_len, 2 * width), jnp.float32),
    )
    query_cot, key_value_cot = in_blocks(
        back_step,
        back_state,
        (
            lax.all_gather(keys_own, "view", axis=0, tiled=True),
            lax.all_gather(values_own, "view", axis=0, tiled=True),
        ),
    )
    own_cot = lax.psum_scatter(key_value_cot, "view", scatter_dimension=0, tiled=True)
    key_cot_own = own_cot[:, :width]
    value_cot_own = own_cot[:, width:]
    projected_cot = jnp.concatenate(
        [query_cot.reshape(rows, width), key_cot_own, value_cot_own], axis=1
    ).astype(jnp.bfloat16)
    input_weight_grad = dot_outer(normed, projected_cot)
    normed_cot = dot_inner(projected_cot, input_weight)
    first_pull = jax.vjp(layer_norm, inputs, gain_one)[1]
    input_part, gain_one_grad = first_pull(normed_cot)
    tokens_grad = (middle_cot + input_part)[None]
    up_part, down_part = (
        lax.psum_scatter(up_grad, ("seq", "view"), scatter_dimension=0, tiled=True),
        lax.psum_scatter(down_grad, ("seq", "view"), scatter_dimension=0, tiled=True),
    )
    summed = lax.psum(
        (gain_one_grad, input_weight_grad, output_weight_grad, gain_two_grad), ("seq", "view")
    )
    return (layer_out, tokens_grad, summed[0], summed[1], summed[2], summed[3], up_part, down_part)


def solution(mesh):
    return jax.shard_map(
        shards,
        mesh=mesh,
        in_specs=(
            P("seq", "view", None),
            P("seq", "view"),
            P("seq", "view"),
            P("seq", "view", None),
            P(),
            P(),
            P(),
            P(),
            P(("seq", "view"), None),
            P(("seq", "view"), None),
        ),
        out_specs=(
            P("seq", "view", None),
            P("seq", "view", None),
            P(),
            P(),
            P(),
            P(),
            P(("seq", "view"), None),
            P(("seq", "view"), None),
        ),
        check_vma=False,
    )
```

profile of v0, /device:TPU:0, one launch (start us, length us, event | category | flops | bytes accessed | tf_op | source)
XLA Modules:
  0.0 1508.5 jit_solution(12384057811492362820)
XLA Ops:
  10.3 4.0 convolution_convert_fusion
  17.6 22.2 %all-gather = s32[1,1024]{1,0:T(1,128)S(1)} all-gather(s32[1,128]{1,0:T(1,128)S(1)} %get-tuple-element.312), channel_id=2, replica_groups=mesh['seq'=4,'view'=8] {'view'}, dimensions={1}, use_global_device_ids=true | all-gather | bytes 4608 | tf_op jit(solution)/shard_map/all_gather | solution.py:91
  39.7 27.6 %all-gather.8.cloned.1.call-done = bf16[1024,1024]{1,0:T(8,128)(2,1)} async-done(((bf16[128,1024]{1,0:T(8,128)(2,1)}), bf16[1024,1024]{1,0:T(8,128)(2,1)}) %all-gather.8.cloned.1.call-update) | async-done | bytes 2097168 | tf_op jit(solution)/shard_map/all_gather | solution.py:135
  67.3 4.0 copy.36
  71.3 46.5 %all-gather.6.cloned.1.call-done = bf16[1024,1024]{1,0:T(8,128)(2,1)} async-done(((bf16[128,1024]{1,0:T(8,128)(2,1)}), bf16[1024,1024]{1,0:T(8,128)(2,1)}) %all-gather.6.cloned.1.call-update) | async-done | bytes 2097168 | tf_op jit(solution)/shard_map/all_gather | solution.py:134
  117.8 3.9 copy.35
  121.8 13.4 while.28
  137.9 58.8 %all-gather.10.cloned.1.call-done = bf16[4096,1024]{1,0:T(8,128)(2,1)} async-done(((bf16[128,1024]{1,0:T(8,128)(2,1)}), bf16[4096,1024]{1,0:T(8,128)(2,1)}) %all-gather.10.cloned.1.call-update) | async-done | bytes 8388624 | tf_op jit(solution)/shard_map/all_gather | solution.py:93
  196.8 7.8 fusion.73
  204.6 71.0 %all-gather.12.cloned.1.call-done = bf16[4096,1024]{1,0:T(8,128)(2,1)} async-done(((bf16[128,1024]{1,0:T(8,128)(2,1)}), bf16[4096,1024]{1,0:T(8,128)(2,1)}) %all-gather.12.cloned.1.call-update) | async-done | bytes 8388624 | tf_op jit(solution)/shard_map/all_gather | solution.py:94
  275.6 10.2 add_convert_fusion
  294.4 4.5 broadcast_in_dim.88
  298.8 32.0 %while.29 = (s32[]{:T(128)}, f32[128,16,64]{0,2,1:T(8,128)S(1)}, f32[1024,2048]{0,1:T(8,128)}, bf16[2,512,1024]{1,2,0:T(8,128)(2,1)}, s32[128]{0:T(128)S(1)}, /*...) while((s32[]{:T(128)}, f32[128,16,64]{0,2,1:T(8,128)S(1)}, ...), condition=%wide.region_12.13_spmd.clone, body=%wide.region_11.12_spmd.clone.sunk | while | flops 686751744 | bytes 104037168 | solution.py:69
  302.8 2.8 fusion.149
  305.6 2.4 fusion.151
  311.5 3.4 copy-done.2
  318.8 2.8 fusion.149
  321.6 2.4 fusion.151
  327.5 3.4 copy-done.2
  331.8 2.7 fusion.78
  334.5 144.5 %reduce-scatter.4.cloned.1.call-done = f32[128,2048]{0,1:T(8,128)} async-done(((f32[1024,2048]{0,1:T(8,128)}), f32[128,2048]{0,1:T(8,128)}) %reduce-scatter.4.cloned.1.call-update) | async-done | bytes 1048592 | tf_op jit(solution)/shard_map/reduce_scatter | solution.py:211
  480.3 6.7 fusion.56
  488.0 11.0 fusion.59
  500.4 8.4 fusion.72
  508.8 10.4 fusion.43
  519.2 5.2 fusion.54
  524.8 41.0 %all-reduce = (f32[1024]{0:T(1024)}, f32[1024]{0:T(1024)}) all-reduce(f32[1024]{0:T(1024)S(1)} %get-tuple-element.248, f32[1024]{0:T(1024)S(1)} %copy-done.19), channel_id=1, replica_groups=mesh['seq'=4,'view'=8] {'seq','view'}, use_global_device_ids=true, to_apply=%region_17.18 | all-reduce | flops 2048 | bytes 16384 | tf_op jit(solution)/shard_map/psum | solution.py:226
  566.9 199.0 %all-reduce.4.cloned.1.call-done = (f32[1024,3072]{1,0:T(8,128)}, f32[1024,1024]{1,0:T(8,128)}) async-done(((f32[1024,3072]{1,0:T(8,128)}, f32[1024,1024]{1,0:T(8,128)}), (f32[1024,3072]{1,0:T(8,128)}, f32[1024,1024]{1,0:T(8,128)})) %all-reduce.4.cloned.1.call-update) | async-done | bytes 16777232 | tf_op jit(solution)/shard_map/psum | solution.py:226
  765.9 360.9 %reduce-scatter.8.cloned.1.call-done = f32[128,1024]{1,0:T(8,128)} async-done(((f32[4096,1024]{1,0:T(8,128)}), f32[128,1024]{1,0:T(8,128)}) %reduce-scatter.8.cloned.1.call-update) | async-done | bytes 524304 | tf_op jit(solution)/shard_map/reduce_scatter | solution.py:224
  1126.9 360.3 %reduce-scatter.6.cloned.1.call-done = f32[128,1024]{1,0:T(8,128)} async-done(((f32[4096,1024]{1,0:T(8,128)}), f32[128,1024]{1,0:T(8,128)}) %reduce-scatter.6.cloned.1.call-update) | async-done | bytes 524304 | tf_op jit(solution)/shard_map/reduce_scatter | solution.py:223
  1487.2 11.1 copy.68
  1498.4 2.1 copy.69
  (151 shorter events, 49.7 us)
Async XLA Ops:
  7.2 129.2 %copy-start = (bf16[1024,1024]{1,0:T(8,128)(2,1)S(1)}, bf16[1024,1024]{1,0:T(8,128)(2,1)}, u32[]{:S(2)}) copy-start(bf16[1024,1024]{1,0:T(8,128)(2,1)} %param.20) | copy-start | bytes 6291460
  7.2 60.2 %all-gather.8.cloned.1.call-start = ((), (), s32[]{:S(2)}) async-start(), calls=%async_computation.4 | async-start | bytes 2359296 | tf_op jit(solution)/shard_map/all_gather | solution.py:135
  9.6 4.7 copy-start.21
  14.3 3.1 copy-start.20
  14.3 3.2 copy-start.23
  14.3 3.2 copy-start.24
  15.2 102.7 %all-gather.6.cloned.1.call-start = ((), (), s32[]{:S(2)}) async-start(), calls=%async_computation.3 | async-start | bytes 2359296 | tf_op jit(solution)/shard_map/all_gather | solution.py:134
  15.9 180.8 %all-gather.10.cloned.1.call-start = ((), (), s32[]{:S(2)}) async-start(), calls=%async_computation.5 | async-start | bytes 8650752 | tf_op jit(solution)/shard_map/all_gather | solution.py:93
  16.7 258.9 %all-gather.12.cloned.1.call-start = ((), (), s32[]{:S(2)}) async-start(), calls=%async_computation.6 | async-start | bytes 8650752 | tf_op jit(solution)/shard_map/all_gather | solution.py:94
  17.3 461.8 %reduce-scatter.4.cloned.1.call-start = ((), (), s32[]{:S(2)}) async-start(), calls=%async_computation.7 | async-start | bytes 9437184 | tf_op jit(solution)/shard_map/reduce_scatter | solution.py:211
  121.8 14.6 copy-start.4
  131.7 1.1 copy-start.15
  275.6 10.2 copy-start.3
  275.6 10.2 copy-start.6
  285.8 2.0 copy-start.8
  285.8 3.1 copy-start.17
  305.5 4.0 slice-start
  308.0 2.2 slice-start.1
  311.4 3.4 copy-start.2
  321.6 4.0 slice-start
  324.0 2.2 slice-start.1
  327.5 3.4 copy-start.2
  330.9 435.1 %all-reduce.4.cloned.1.call-start = ((), (), s32[]{:S(2)}) async-start(), calls=%async_computation.10 | async-start | bytes 33554432 | tf_op jit(solution)/shard_map/psum | solution.py:226
  487.1 639.8 %reduce-scatter.8.cloned.1.call-start = ((), (), s32[]{:S(2)}) async-start(), calls=%async_computation.9 | async-start | bytes 17301504 | tf_op jit(solution)/shard_map/reduce_scatter | solution.py:224
  499.0 1.1 copy-start.7
  499.0 1.4 copy-start.9
  499.1 988.2 %reduce-scatter.6.cloned.1.call-start = ((), (), s32[]{:S(2)}) async-start(), calls=%async_computation.8 | async-start | bytes 17301504 | tf_op jit(solution)/shard_map/reduce_scatter | solution.py:223
  519.2 5.2 copy-start.22
  519.2 5.6 copy-start.19
  519.2 46.6 %copy-start.11 = (f32[128,1024]{1,0:T(8,128)S(1)}, f32[128,1024]{1,0:T(8,128)}, u32[]{:S(2)}) copy-start(f32[128,1024]{1,0:T(8,128)} %copy-done.10) | copy-start | bytes 1572868
  1487.2 11.1 copy-start.12
  1498.4 3.1 copy-start.1
  (8 other events, 7.3 us)
Sparse Core Ops, SparseCore 0:
  15.3 51.9 all-gather.7
  70.0 47.7 all-gather.5
  120.8 75.8 all-gather.9
  199.6 75.9 all-gather.11
  331.0 147.9 reduce-scatter.3
  487.2 278.6 all-reduce.3
  768.9 357.9 reduce-scatter.7
  1129.9 357.3 reduce-scatter.5
where the time goes:
time: 1520 us; the launch traced here: 1510 us
  waiting for transfers between devices  1270 us (84%)
  matrix products  90.6 us (6%)
  blocking collectives  63.2 us (4%)
  local copies, waits for them, and re-layouts  52.1 us (3%)
    reduce_scatter x1, waiting for transfers between devices, shards(): lax.psum_scatter(down_grad, ('seq', 'view'), scatter_dimension=0, tiled=T...  361 us
    reduce_scatter x1, waiting for transfers between devices, shards(): lax.psum_scatter(up_grad, ('seq', 'view'), scatter_dimension=0, tiled=True)  360 us
    psum x1, waiting for transfers between devices, shards(): lax.psum((gain_one_grad, input_weight_grad, output_weight_grad, gain_two_...  199 us
    reduce_scatter x1, waiting for transfers between devices, shards(): lax.psum_scatter(key_value_cot, 'view', scatter_dimension=0, tiled=True)  145 us
    all_gather x1, waiting for transfers between devices, shards(): lax.all_gather(down_weight, ('seq', 'view'), axis=0, tiled=True)  71 us
    all_gather x1, waiting for transfers between devices, shards(): lax.all_gather(up_weight, ('seq', 'view'), axis=0, tiled=True)  58.8 us
    all_gather x1, waiting for transfers between devices, shards(): lax.all_gather(keys_own, 'view', axis=0, tiled=True)  46.5 us
    psum x1, blocking collectives, shards(): lax.psum((gain_one_grad, input_weight_grad, output_weight_grad, gain_two_...  41 us
  transfers between devices with their start and end apart: 8, of which 8 were waited for; matrix products, arithmetic and copies ran while one was open for 5% of the time, Pallas kernels for 0%

commit v1 on v0

--- a/solution.py
+++ b/solution.py
@@ -1,8 +1,12 @@
+import functools
 import math
+import types
 
 import jax
 import jax.numpy as jnp
 from jax import lax
+from jax.experimental import pallas as pl
+from jax.experimental.pallas import tpu as pltpu
 from jax.sharding import PartitionSpec as P
 
 HEADS = 16
@@ -11,6 +15,9 @@
 
 EPS = 1e-05
 NEGATIVE = -1e30
+MESH = pl.DeviceIdType.MESH
+SLOTS = 4
+SCENE_BLOCKS = 16
 
 
 def layer_norm(values, gain):
@@ -229,9 +236,690 @@
     return (layer_out, tokens_grad, summed[0], summed[1], summed[2], summed[3], up_part, down_part)
 
 
+def dot_nn(left, right):
+    return lax.dot_general(left, right, (((1,), (0,)), ((), ())), preferred_element_type=jnp.float32)
+
+
+def at(start, size):
+    return pl.ds(pl.multiple_of(start, size), size)
+
+
+def norm_stats(values):
+    mean = jnp.mean(values, axis=-1, keepdims=True)
+    center = values - mean
+    spread = jnp.mean(center * center, axis=-1, keepdims=True)
+    inverse = lax.rsqrt(spread + EPS)
+    return center * inverse, inverse
+
+
+def norm_back(cot, unit, inverse, gain):
+    scaled = cot * gain
+    first = jnp.mean(scaled, axis=-1, keepdims=True)
+    second = jnp.mean(scaled * unit, axis=-1, keepdims=True)
+    return inverse * (scaled - first - unit * second)
+
+
+class Wires:
+    def __init__(self, send_sem, recv_sem, peer):
+        self.send_sem, self.recv_sem, self.peer = send_sem, recv_sem, peer
+        self.sends, self.recvs, self.pending = 0, 0, []
+
+    def inbox(self, count):
+        base = self.recvs
+        self.recvs += count
+        return base
+
+    def send(self, src, dst, slot, device):
+        copy = pltpu.make_async_remote_copy(
+            src_ref=src,
+            dst_ref=dst,
+            send_sem=self.send_sem.at[self.sends],
+            recv_sem=self.recv_sem.at[slot],
+            device_id=device,
+            device_id_type=MESH,
+        )
+        self.sends += 1
+        copy.start()
+        self.pending.append(copy)
+        return copy
+
+    def sent(self, copy):
+        copy.wait_send()
+        self.pending = [other for other in self.pending if other is not copy]
+
+    def wait(self, dst, slot):
+        pltpu.make_async_remote_copy(
+            src_ref=dst,
+            dst_ref=dst,
+            send_sem=self.send_sem.at[0],
+            recv_sem=self.recv_sem.at[slot],
+            device_id=self.peer,
+            device_id_type=MESH,
+        ).wait_recv()
+
+    def drain(self):
+        for copy in self.pending:
+            copy.wait_send()
+
+
+SENDS, RECVS, LOCALS = 200, 200, 24
+
+
+def scratch_of(rows, width, seqs, views, hidden):
+    length = rows * views
+    own = width // views
+    bf, f3 = jnp.bfloat16, jnp.float32
+    vm = pltpu.VMEM
+    mlp_rows = hidden * seqs * views // 4
+    return dict(
+        w_full=vm((width, 3 * width), bf),
+        w_own=vm((width, 3 * own), bf),
+        wo=vm((width, width), bf),
+        up=vm((mlp_rows, width), bf),
+        down=vm((mlp_rows, width), bf),
+        ids_all=vm((views, 8, 128), jnp.int32),
+        order_vm=vm((16, 128), jnp.int32),
+        order_sm=pltpu.SMEM((16, 128), jnp.int32),
+        normed=vm((length, width), bf),
+        qkv=vm((length, 3 * own), bf),
+        qkv_s=vm((length, 3 * own), bf),
+        weights=vm((2 * SLOTS, length // SLOTS, length // SLOTS), f3),
+        totals=vm((2 * SLOTS, length // SLOTS, 1), f3),
+        att_s=vm((length, own), f3),
+        att=vm((length, own), bf),
+        att_tok=vm((rows, width), bf),
+        middle=vm((rows, width), f3),
+        normed_two=vm((4 * rows, width), bf),
+        mixed_cot=vm((4 * rows, width), bf),
+        act_cot=vm((4 * rows, mlp_rows), f3),
+        act=vm((4 * rows, mlp_rows), bf),
+        hid_cot=vm((4 * rows, mlp_rows), bf),
+        part_own=vm((2, rows, width), f3),
+        part_out=vm((2, 3, rows, width), bf),
+        part_in=vm((2, 4, rows, width), bf),
+        grad_keep=vm((2, mlp_rows // 2, width), bf),
+        grad_pass=vm((2, mlp_rows // 2, width), bf),
+        grad_core=vm((2, mlp_rows // 2, width), bf),
+        grad_in=vm((2, 4, hidden, width), bf),
+        branch=vm((length, width), bf),
+        acot_tok=vm((rows, width), bf),
+        acot=vm((length, own), bf),
+        acot_s=vm((length, own), bf),
+        pc_s=vm((length, 3 * own), bf),
+        pc=vm((3, length, own), bf),
+        pc_tok=vm((3, rows, width), bf),
+        dw_out=vm((3, 3, width // seqs, own), bf),
+        dw_in=vm((4, 3, width // seqs, own), bf),
+        do_out=vm((own, width), bf),
+        do_in=vm((4, own // seqs, width), bf),
+        fin_w=vm((3, width, width), bf),
+        fin_o=vm((width, width), bf),
+        gain_own=vm((8, width), f3),
+        gain_in=vm((seqs, 8, width), f3),
+        gain_sum=vm((8, width), f3),
+        gain_all=vm((views, 8, width), f3),
+        send_sem=pltpu.SemaphoreType.DMA((SENDS,)),
+        recv_sem=pltpu.SemaphoreType.DMA((RECVS,)),
+        local_sem=pltpu.SemaphoreType.DMA((LOCALS,)),
+    )
+
+
+def layer_kernel(names, seqs, views, *refs):
+    (tok, ids, alive, out_cot, gain_one_ref, gain_two_ref, w_hbm, wo_hbm, up_hbm, down_hbm) = refs[:10]
+    (layer_out, tokens_grad, gains, w_grad, o_grad, up_grad, down_grad) = refs[10:17]
+    k = types.SimpleNamespace(**dict(zip(names, refs[17:])))
+    rows, width = tok.shape
+    length = rows * views
+    own = width // views
+    hidden = up_hbm.shape[0]
+    mlp_rows = k.up.shape[0]
+    half = mlp_rows // 2
+    levels = views // 2
+    block = length // (SLOTS * SCENE_BLOCKS)
+    scene = length // SLOTS
+    scale = HEAD_DIM ** (-0.5)
+    bf, f3 = jnp.bfloat16, jnp.float32
+
+    s = lax.axis_index("seq")
+    v = lax.axis_index("view")
+    x, c, z, y = s // 2, s % 2, v // 2, v % 2
+    x_s, c_s, xc_s = (1 - x) * 2 + c, x * 2 + (1 - c), (1 - x) * 2 + (1 - c)
+    y_v = z * 2 + (1 - y)
+    others_z = [lax.rem(z + d, levels) for d in range(1, levels)]
+    group = [(x_s, v), (s, y_v), (x_s, y_v)]
+    group_slot = [(1 - x) * 2 + y, x * 2 + (1 - y), (1 - x) * 2 + (1 - y)]
+    own_slot = x * 2 + y
+    view_peers = [lax.rem(v + d, views) for d in range(1, views)]
+    seq_peers = [x_s, xc_s, c_s]
+
+    wires = Wires(k.send_sem, k.recv_sem, (c_s, v))
+    in_normed = wires.inbox(views)
+    in_ids = wires.inbox(views)
+    in_up = wires.inbox(levels + 1)
+    in_down = wires.inbox(levels + 1)
+    in_mcot = wires.inbox(4)
+    in_att = wires.inbox(views)
+    in_two = wires.inbox(4)
+    in_part = [wires.inbox(4), wires.inbox(4)]
+    in_core = [wires.inbox(1), wires.inbox(1)]
+    in_grad = [wires.inbox(levels), wires.inbox(levels)]
+    in_acot = wires.inbox(views)
+    in_branch = wires.inbox(views)
+    in_pc = wires.inbox(views)
+    in_dw = wires.inbox(seqs)
+    in_do = wires.inbox(seqs)
+    in_fw = wires.inbox(seqs * views)
+    in_fo = wires.inbox(seqs * views)
+    in_gain = wires.inbox(seqs)
+    in_gains = wires.inbox(views)
+
+    loads = []
+
+    def load(src, dst):
+        copy = pltpu.make_async_copy(src, dst, k.local_sem.at[len(loads)])
+        copy.start()
+        loads.append(copy)
+        return copy
+
+    up_slot = at((c * levels + z) * hidden, hidden)
+    load_up = load(up_hbm, k.up.at[up_slot])
+    load_down = load(down_hbm, k.down.at[up_slot])
+    load_own = [
+        load(w_hbm.at[:, at(t * width + v * own, own)], k.w_own.at[:, pl.ds(t * own, own)])
+        for t in range(3)
+    ]
+    load_wo = load(wo_hbm, k.wo)
+    load_w = load(w_hbm, k.w_full)
+
+    barrier = pltpu.get_barrier_semaphore()
+    greeted = [(s, p) for p in view_peers] + [(p, v) for p in seq_peers] + [(x_s, y_v)]
+    for device in greeted:
+        pl.semaphore_signal(barrier, inc=1, device_id=device, device_id_type=MESH)
+
+    gain_one = gain_one_ref[...].astype(f3)
+    gain_two = gain_two_ref[...].astype(f3)
+    unit, _ = norm_stats(tok[...].astype(f3))
+    k.normed[at(v * rows, rows), :] = (unit * gain_one).astype(bf)
+    per = rows // block
+    lane = lax.broadcasted_iota(jnp.int32, (1, 128), 1)
+    scenes = jnp.zeros((1, 128), jnp.int32)
+    for m in range(per):
+        mine = jnp.broadcast_to(ids[:, m * block : m * block + 1], (1, 128))
+        scenes = jnp.where(lane == v * per + m, mine, scenes)
+    k.ids_all[v] = jnp.broadcast_to(scenes, (8, 128))
+    live = jnp.transpose(jnp.broadcast_to(alive[...].astype(f3), (rows, rows)))[:, :1]
+    k.mixed_cot[at(own_slot * rows, rows), :] = (live * out_cot[...].astype(f3)).astype(bf)
+    pl.semaphore_wait(barrier, len(greeted))
+
+    def view_rows(ref, j):
+        return ref.at[at(j * rows, rows)]
+
+    for p in view_peers:
+        wires.send(k.ids_all.at[v], k.ids_all.at[v], in_ids + v, (s, p))
+    wires.send(view_rows(k.normed, v), view_rows(k.normed, v), in_normed + v, (s, y_v))
+    for zt in others_z:
+        wires.send(view_rows(k.normed, v), view_rows(k.normed, v), in_normed + v, (s, zt * 2 + y))
+
+    def send_mlp_rows(ref, base):
+        for zt in others_z:
+            wires.send(ref.at[up_slot], ref.at[up_slot], base + z, (s, zt * 2 + y))
+
+    load_up.wait()
+    send_mlp_rows(k.up, in_up)
+
+    for p in view_peers:
+        wires.wait(k.ids_all.at[p], in_ids + p)
+    count = SLOTS * SCENE_BLOCKS
+    scene_row = k.ids_all[0][:1]
+    for j in range(1, views):
+        scene_row = scene_row + k.ids_all[j][:1]
+    big = lax.broadcasted_iota(jnp.int32, (128, 128), 0)
+    wide = lax.broadcasted_iota(jnp.int32, (128, 128), 1)
+    scene_mat = jnp.broadcast_to(scene_row, (128, 128))
+    scene_col = jnp.transpose(scene_mat)
+    ahead = (scene_col < scene_mat) | ((scene_col == scene_mat) & (big < wide))
+    place = jnp.sum(jnp.where(ahead & (big < count), 1, 0), axis=0, keepdims=True)
+    place_col = jnp.transpose(jnp.broadcast_to(place, (128, 128)))
+    hit = jnp.where((place_col == wide) & (big < count), big, 0)
+    source = jnp.sum(hit, axis=0, keepdims=True)
+    k.order_vm[0:8, :] = jnp.broadcast_to(source, (8, 128))
+    k.order_vm[8:16, :] = jnp.broadcast_to(place, (8, 128))
+    to_scalar = load(k.order_vm, k.order_sm)
+
+    for copy in load_own:
+        copy.wait()
+
+    def project(j):
+        k.qkv[at(j * rows, rows), :] = dot_nn(k.normed[at(j * rows, rows), :], k.w_own[...]).astype(bf)
+
+    project(v)
+    for zt in others_z:
+        j = zt * 2 + y
+        wires.wait(view_rows(k.normed, j), in_normed + j)
+        wires.send(view_rows(k.normed, j), view_rows(k.normed, j), in_normed + j, (s, y_v))
+        project(j)
+    for zt in [z] + others_z:
+        j = zt * 2 + 1 - y
+        wires.wait(view_rows(k.normed, j), in_normed + j)
+        project(j)
+    to_scalar.wait()
+
+    def reorder(dst, src, row):
+        blocks = src.reshape(count, block, src.shape[1])
+
+        def step(i, unused):
+            from_block = k.order_sm[row, i]
+            dst[at(i * block, block), :] = blocks[from_block].astype(dst.dtype)
+            return unused
+
+        lax.fori_loop(0, count, step, 0, unroll=8)
+
+    reorder(k.qkv_s, k.qkv, 0)
+
+    head_lane = lax.broadcasted_iota(jnp.int32, (scene, own), 1) // HEAD_DIM
+
+    def attend(g, unused):
+        here = at(g * scene, scene)
+        queries, keys, values = (k.qkv_s[here, pl.ds(t * own, own)] for t in range(3))
+        result = jnp.zeros((scene, own), f3)
+        for e in range(2):
+            chosen = jnp.where(head_lane == e, queries, jnp.zeros_like(queries))
+            weights = jnp.exp(dot_inner(chosen, keys) * scale)
+            total = jnp.sum(weights, axis=-1, keepdims=True)
+            k.weights[g * 2 + e] = weights
+            k.totals[g * 2 + e] = total
+            mixed = dot_nn(weights.astype(bf), values) / total
+            result = jnp.where(head_lane == e, mixed, result)
+        k.att_s[here, :] = result
+        return unused
+
+    lax.fori_loop(0, SLOTS, attend, 0)
+    reorder(k.att, k.att_s, 8)
+    own_cols = at(v * own, own)
+    for p in view_peers:
+        wires.send(view_rows(k.att, p), k.att_tok.at[:, own_cols], in_att + v, (s, p))
+    k.att_tok[:, own_cols] = k.att[at(v * rows, rows), :]
+
+    load_down.wait()
+    send_mlp_rows(k.down, in_down)
+    mcot_own = at(own_slot * rows, rows)
+    for device in group:
+        wires.send(k.mixed_cot.at[mcot_own], k.mixed_cot.at[mcot_own], in_mcot + own_slot, device)
+
+    def core_exchange(ref, base):
+        for zt in others_z:
+            there = at((c * levels + zt) * hidden, hidden)
+            wires.wait(ref.at[there], base + zt)
+        mine = at(c * half, half)
+        wires.send(ref.at[mine], ref.at[mine], base + levels, (c_s, v))
+
+    core_exchange(k.up, in_up)
+
+    load_wo.wait()
+    for p in view_peers:
+        wires.wait(k.att_tok.at[:, at(p * own, own)], in_att + p)
+    tile = 256
+    for n in range(width // tile):
+        cols = pl.ds(n * tile, tile)
+        k.middle[:, cols] = tok[:, cols].astype(f3) + live * dot_nn(k.att_tok[...], k.wo[:, cols])
+    unit_two, _ = norm_stats(k.middle[...])
+    k.normed_two[mcot_own, :] = (unit_two * gain_two).astype(bf)
+    for device in group:
+        wires.send(k.normed_two.at[mcot_own], k.normed_two.at[mcot_own], in_two + own_slot, device)
+
+    for slot in group_slot:
+        there = at(slot * rows, rows)
+        wires.wait(k.mixed_cot.at[there], in_mcot + slot)
+    core_exchange(k.down, in_down)
+    theirs = at((1 - c) * half, half)
+    wires.wait(k.up.at[theirs], in_up + levels)
+    wires.wait(k.down.at[theirs], in_down + levels)
+
+    def cot_tile(n, unused):
+        k.act_cot[:, at(n * tile, tile)] = dot_inner(k.mixed_cot[...], k.down[at(n * tile, tile), :])
+        return unused
+
+    lax.fori_loop(0, mlp_rows // tile, cot_tile, 0)
+
+    def mlp_tile(slot):
+        here = at(slot * rows, rows)
+
+        def step(n, unused):
+            cols = at(n * tile, tile)
+            pre = dot_inner(k.normed_two[here, :], k.up[cols, :])
+            below = 0.5 + 0.5 * lax.erf(pre * (0.5**0.5))
+            slope = below + pre * (jnp.exp(-0.5 * pre * pre) * (0.5 / math.pi) ** 0.5)
+            k.act[here, cols] = (pre * below).astype(bf)
+            k.hid_cot[here, cols] = (k.act_cot[here, cols] * slope).astype(bf)
+            return unused
+
+        lax.fori_loop(0, mlp_rows // tile, step, 0)
+
+    def part_tiles(which, left, right, slot, dst):
+        here = at(slot * rows, rows)
+
+        def step(n, unused):
+            cols = at(n * tile, tile)
+            dst[:, cols] = dot_nn(left[here, :], right[:, cols]).astype(dst.dtype)
+            return unused
+
+        lax.fori_loop(0, width // tile, step, 0)
+
+    mlp_tile(own_slot)
+    for i, (slot, device) in enumerate(zip(group_slot, group)):
+        wires.wait(k.normed_two.at[at(slot * rows, rows)], in_two + slot)
+        mlp_tile(slot)
+        part_tiles(0, k.hid_cot, k.up, slot, k.part_out.at[0, i])
+        wires.send(k.part_out.at[0, i], k.part_in.at[0, own_slot], in_part[0] + own_slot, device)
+    part_tiles(0, k.hid_cot, k.up, own_slot, k.part_own.at[0])
+
+    def grad_tiles(left, right, start, dst):
+        def step(n, unused):
+            there = at(n * tile, tile)
+            dst[there, :] = dot_outer(left[:, at(start + n * tile, tile)], right[...]).astype(dst.dtype)
+            return unused
+
+        lax.fori_loop(0, half // tile, step, 0)
+
+    pairs = ((k.act, k.mixed_cot), (k.hid_cot, k.normed_two))
+    passed = []
+    for which, (left, right) in enumerate(pairs):
+        grad_tiles(left, right, (1 - c) * half, k.grad_pass.at[which])
+        passed.append(wires.send(k.grad_pass.at[which], k.grad_core.at[which], in_core[which], (c_s, v)))
+    for which, (left, right) in enumerate(pairs):
+        grad_tiles(left, right, c * half, k.grad_keep.at[which])
+
+    def part_sum(which):
+        total = k.part_own[which]
+        for slot in group_slot:
+            wires.wait(k.part_in.at[which, slot], in_part[which] + slot)
+            total = total + k.part_in[which, slot].astype(f3)
+        return total
+
+    unit_two, inverse_two = norm_stats(k.middle[...])
+    cot_two = part_sum(0)
+    k.gain_own[1:2, :] = jnp.sum(cot_two * unit_two, axis=0, keepdims=True)
+    middle_cot = out_cot[...].astype(f3) + norm_back(cot_two, unit_two, inverse_two, gain_two)
+    tokens_grad[...] = middle_cot
+    k.branch[at(v * rows, rows), :] = (live * middle_cot).astype(bf)
+    for n in range(width // tile):
+        k.acot_tok[:, pl.ds(n * tile, tile)] = dot_inner(
+            k.branch[at(v * rows, rows), :], k.wo[pl.ds(n * tile, tile), :]
+        ).astype(bf)
+    for p in view_peers:
+        wires.send(k.acot_tok.at[:, at(p * own, own)], view_rows(k.acot, v), in_acot + v, (s, p))
+    k.acot[at(v * rows, rows), :] = k.acot_tok[:, own_cols]
+    wires.send(view_rows(k.branch, v), view_rows(k.branch, v), in_branch + v, (s, y_v))
+    for zt in others_z:
+        wires.send(view_rows(k.branch, v), view_rows(k.branch, v), in_branch + v, (s, zt * 2 + y))
+
+    def grad_level(which, zt):
+        there = at(zt * hidden, hidden)
+        return k.grad_keep[which, there, :].astype(f3) + k.grad_core[which, there, :].astype(f3)
+
+    for which in range(2):
+        wires.wait(k.grad_core.at[which], in_core[which])
+        wires.sent(passed[which])
+        for zt in others_z:
+            k.grad_pass[which, at(zt * hidden, hidden), :] = grad_level(which, zt).astype(bf)
+
+    def send_grads(which):
+        for zt in others_z:
+            wires.send(
+                k.grad_pass.at[which, at(zt * hidden, hidden)],
+                k.grad_in.at[which, z],
+                in_grad[which] + z,
+                (s, zt * 2 + y),
+            )
+
+    send_grads(0)
+
+    for i, (slot, device) in enumerate(zip(group_slot, group)):
+        part_tiles(1, k.act, k.down, slot, k.part_out.at[1, i])
+        wires.send(k.part_out.at[1, i], k.part_in.at[1, own_slot], in_part[1] + own_slot, device)
+    part_tiles(1, k.act, k.down, own_slot, k.part_own.at[1])
+
+    for p in view_peers:
+        wires.wait(view_rows(k.acot, p), in_acot + p)
+    reorder(k.acot_s, k.acot, 0)
+
+    def attend_back(g, unused):
+        here = at(g * scene, scene)
+        queries, keys, values = (k.qkv_s[here, pl.ds(t * own, own)] for t in range(3))
+        cots = k.acot_s[here, :]
+        agree = cots.astype(f3) * k.att_s[here, :]
+        outs = [jnp.zeros((scene, own), f3) for t in range(3)]
+        for e in range(2):
+            mine = head_lane == e
+            delta = jnp.sum(jnp.where(mine, agree, 0.0), axis=-1, keepdims=True)
+            chosen = jnp.where(mine, cots, jnp.zeros_like(cots))
+            weights = k.weights[g * 2 + e]
+            inverse = 1.0 / k.totals[g * 2 + e]
+            weights_cot = dot_inner(chosen, values)
+            score_cot = (weights * inverse * (weights_cot - delta)).astype(bf)
+            shared = (cots.astype(f3) * inverse).astype(bf)
+            new = (
+                dot_nn(score_cot, keys) * scale,
+                dot_outer(score_cot, queries) * scale,
+                dot_outer(weights.astype(bf), shared),
+            )
+            outs = [jnp.where(mine, fresh, old) for fresh, old in zip(new, outs)]
+        for t in range(3):
+            k.pc_s[here, pl.ds(t * own, own)] = outs[t].astype(bf)
+        return unused
+
+    lax.fori_loop(0, SLOTS, attend_back, 0)
+
+    pc_blocks = k.pc_s.reshape(count, block, 3 * own)
+
+    def unsort(i, unused):
+        found = pc_blocks[k.order_sm[8, i]]
+        for t in range(3):
+            k.pc[t, at(i * block, block), :] = found[:, t * own : (t + 1) * own]
+        return unused
+
+    lax.fori_loop(0, count, unsort, 0, unroll=8)
+    for p in view_peers:
+        wires.send(k.pc.at[:, at(p * rows, rows)], k.pc_tok.at[:, :, own_cols], in_pc + v, (s, p))
+    for t in range(3):
+        k.pc_tok[t, :, own_cols] = k.pc[t, at(v * rows, rows), :]
+    send_grads(1)
+
+    for zt in others_z:
+        j = zt * 2 + y
+        wires.wait(view_rows(k.branch, j), in_branch + j)
+        wires.send(view_rows(k.branch, j), view_rows(k.branch, j), in_branch + j, (s, y_v))
+
+    part = width // seqs
+    for i, p in enumerate(seq_peers):
+        for t in range(3):
+            k.dw_out[i, t] = dot_outer(k.normed[:, at(p * part, part)], k.pc[t]).astype(bf)
+        wires.send(k.dw_out.at[i], k.dw_in.at[s], in_dw + s, (p, v))
+    for zt in [z] + others_z:
+        j = zt * 2 + 1 - y
+        wires.wait(view_rows(k.branch, j), in_branch + j)
+    for n in range(width // tile):
+        cols = pl.ds(n * tile, tile)
+        k.do_out[:, cols] = dot_outer(k.att[...], k.branch[:, cols]).astype(bf)
+    piece = own // seqs
+    for p in seq_peers:
+        wires.send(k.do_out.at[at(p * piece, piece)], k.do_in.at[s], in_do + s, (p, v))
+    own_part = at(s * part, part)
+    own_dw = [dot_outer(k.normed[:, own_part], k.pc[t]) for t in range(3)]
+    for p in seq_peers:
+        wires.wait(k.dw_in.at[p], in_dw + p)
+    for t in range(3):
+        total = own_dw[t]
+        for p in seq_peers:
+            total = total + k.dw_in[p, t].astype(f3)
+        k.fin_w[t, own_part, own_cols] = total.astype(bf)
+    for p in seq_peers:
+        wires.wait(k.do_in.at[p], in_do + p)
+    total = k.do_out[at(s * piece, piece), :].astype(f3)
+    for p in seq_peers:
+        total = total + k.do_in[p].astype(f3)
+
+    def fin_w(q, j):
+        return k.fin_w.at[:, at(q * part, part), at(j * own, own)]
+
+    def fin_o(q, j):
+        return k.fin_o.at[at(j * own + q * piece, piece)]
+
+    k.fin_o[at(v * own + s * piece, piece), :] = total.astype(bf)
+
+    def pass_on(q, j, device):
+        wires.send(fin_w(q, j), fin_w(q, j), in_fw + q * views + j, device)
+        wires.send(fin_o(q, j), fin_o(q, j), in_fo + q * views + j, device)
+
+    def arrive(q, j):
+        wires.wait(fin_w(q, j), in_fw + q * views + j)
+        wires.wait(fin_o(q, j), in_fo + q * views + j)
+
+    pass_on(s, v, (s, y_v))
+    for zt in others_z:
+        pass_on(s, v, (s, zt * 2 + y))
+    pass_on(s, v, (x_s, v))
+    pass_on(s, v, (c_s, v))
+
+    load_w.wait()
+    for p in view_peers:
+        wires.wait(k.pc_tok.at[:, :, at(p * own, own)], in_pc + p)
+
+    def back_tile(n, unused):
+        cols = at(n * tile, tile)
+        total = dot_inner(k.pc_tok[0], k.w_full[cols, pl.ds(0, width)])
+        for t in range(1, 3):
+            total = total + dot_inner(k.pc_tok[t], k.w_full[cols, pl.ds(t * width, width)])
+        k.part_own[0, :, cols] = total
+        return unused
+
+    lax.fori_loop(0, width // tile, back_tile, 0)
+    unit_one, inverse_one = norm_stats(tok[...].astype(f3))
+    cot_one = k.part_own[0]
+    k.gain_own[0:1, :] = jnp.sum(cot_one * unit_one, axis=0, keepdims=True)
+    k.gain_own[2:8, :] = jnp.zeros((6, width), f3)
+    tokens_grad[...] = tokens_grad[...] + norm_back(cot_one, unit_one, inverse_one, gain_one)
+    for p in seq_peers:
+        wires.send(k.gain_own, k.gain_in.at[s], in_gain + s, (p, v))
+
+    for zt in others_z:
+        j = zt * 2 + y
+        arrive(s, j)
+        for device in ((s, y_v), (x_s, v), (c_s, v)):
+            pass_on(s, j, device)
+    for zt in [z] + others_z:
+        j = zt * 2 + 1 - y
+        arrive(s, j)
+        for device in ((x_s, v), (c_s, v)):
+            pass_on(s, j, device)
+
+    total = k.gain_own[...]
+    for p in seq_peers:
+        wires.wait(k.gain_in.at[p], in_gain + p)
+        total = total + k.gain_in[p]
+    k.gain_sum[...] = total
+    for p in view_peers:
+        wires.send(k.gain_sum, k.gain_all.at[v], in_gains + v, (s, p))
+
+    layer_out[...] = (k.middle[...] + live * part_sum(1)).astype(bf)
+    for which, dst in enumerate((down_grad, up_grad)):
+        total = grad_level(which, z)
+        for zt in others_z:
+            wires.wait(k.grad_in.at[which, zt], in_grad[which] + zt)
+            total = total + k.grad_in[which, zt].astype(f3)
+        dst[...] = total
+
+    total = k.gain_sum[...]
+    for p in view_peers:
+        wires.wait(k.gain_all.at[p], in_gains + p)
+        total = total + k.gain_all[p]
+    gains[...] = total
+
+    for j in [v, y_v] + [p for zt in others_z for p in (zt * 2 + y, zt * 2 + 1 - y)]:
+        arrive(x_s, j)
+        pass_on(x_s, j, (c_s, v))
+    for j in range(views):
+        arrive(c_s, j)
+        arrive(xc_s, j)
+    out_w = pltpu.make_async_copy(k.fin_w, w_grad, k.local_sem.at[LOCALS - 1])
+    out_o = pltpu.make_async_copy(k.fin_o, o_grad, k.local_sem.at[LOCALS - 2])
+    out_w.start()
+    out_o.start()
+    wires.drain()
+    out_w.wait()
+    out_o.wait()
+
+
+def fused(
+    seqs,
+    views,
+    tokens,
+    scene_ids,
+    live_mask,
+    out_grad,
+    attention_gain,
+    input_weight,
+    output_weight,
+    feedforward_gain,
+    up_weight,
+    down_weight,
+):
+    rows, width = tokens.shape[1:]
+    hidden = up_weight.shape[0]
+    spec = scratch_of(rows, width, seqs, views, hidden)
+    vmem = pl.BlockSpec(memory_space=pltpu.VMEM)
+    anywhere = pl.BlockSpec(memory_space=pl.ANY)
+    shape = jax.ShapeDtypeStruct
+    bf, f3 = jnp.bfloat16, jnp.float32
+    layer_out, tokens_grad, gains, w_grad, o_grad, up_grad, down_grad = pl.pallas_call(
+        functools.partial(layer_kernel, tuple(spec), seqs, views),
+        out_shape=(
+            shape((rows, width), bf),
+            shape((rows, width), f3),
+            shape((8, width), f3),
+            shape((3, width, width), bf),
+            shape((width, width), bf),
+            shape((hidden, width), f3),
+            shape((hidden, width), f3),
+        ),
+        in_specs=[vmem] * 6 + [anywhere] * 4,
+        out_specs=(vmem, vmem, vmem, anywhere, anywhere, vmem, vmem),
+        scratch_shapes=list(spec.values()),
+        compiler_params=pltpu.CompilerParams(
+            collective_id=0, has_side_effects=True, vmem_limit_bytes=67043328
+        ),
+        name="layer",
+    )(
+        tokens[0],
+        scene_ids,
+        live_mask,
+        out_grad[0],
+        attention_gain[None],
+        feedforward_gain[None],
+        input_weight,
+        output_weight,
+        up_weight,
+        down_weight,
+    )
+    wide = jnp.concatenate([w_grad[t].astype(f3) for t in range(3)], axis=1)
+    return (
+        layer_out[None],
+        tokens_grad[None],
+        gains[0],
+        wide,
+        o_grad.astype(f3),
+        gains[1],
+        up_grad,
+        down_grad,
+    )
+
+
 def solution(mesh):
+    seqs, views = mesh.shape["seq"], mesh.shape["view"]
+    small = seqs == 4 and views % 2 == 0 and HEADS == 2 * views
+    body = functools.partial(fused, seqs, views) if small else shards
     return jax.shard_map(
-        shards,
+        body,
         mesh=mesh,
         in_specs=(
             P("seq", "view", None),

time: 1520 us -> 284 us (0.19)
  the two profiles are of different devices: /device:TPU:0 before, /device:TPU:13 now
where the time goes in v1:
time: 284 us
  Pallas kernels  265 us (93%)
  local copies, waits for them, and re-layouts  10.7 us (4%)
  other arithmetic  7.66 us (3%)
    pallas_call x1, Pallas kernels, fused(): pl.pallas_call(functools.partial(layer_kernel, tuple(spec), seqs, views),...  265 us

profile of v1, /device:TPU:13, one launch (start us, length us, event | category | flops | bytes accessed | tf_op | source)
XLA Modules:
  0.0 283.6 jit_solution(7862531257044814000)
XLA Ops:
  0.6 1.3 broadcast_in_dim.12.refs_4_
  1.9 1.3 broadcast_in_dim.13.refs_5_
  3.2 264.7 %layer.1 = (bf16[128,1024]{1,0:T(8,128)(2,1)}, f32[128,1024]{1,0:T(8,128)}, f32[8,1024]{1,0:T(8,128)}, bf16[3,1024,1024]{2,1,0:T(8,128)(2,1)}, bf16[1024,1024]{1...) custom-call(bf16[128,1024]{1,0:T(8,128)(2,1)} %bitcast.13, s32[1,128]{1,0:T(1,128)} %refs_1_.1, ...), custom_call_target="tpu_custom_call" | custom-call | tf_op jit(solution)/shard_map/layer/pallas_call | solution.py:874
  267.8 1.4 fusion
  269.3 3.6 %slice_bitcast_fusion.2 = (bf16[1024,1024]{1,0:T(8,128)(2,1)S(1)}, bf16[1024,1024]{1,0:T(8,128)(2,1)S(1)}, bf16[1024,1024]{1,0:T(8,128)(2,1)S(1)}) fusion(bf16[3,1024,1024]{2,1,0:T(8,128)(2,1)} %get-tuple-element.18), kind=kLoop, calls=%fused_computation.3 | loop fusion | bytes 12582912 | tf_op jit(solution)/shard_map/convert_element_type | solution.py:904
  272.9 0.0 copy-start
  272.9 5.2 %maximum_convert_fusion = f32[1024,3072]{1,0:T(8,128)} fusion(bf16[1024,1024]{1,0:T(8,128)(2,1)S(1)} %get-tuple-element.23, bf16[1024,1024]{1,0:T(8,128)(2,1)S(1)} %get-tuple-element.24, bf16[1024,1024]{1,0:T(8,128)(2,1)S(1)} %get-tuple-element.22), kind=kLoop, calls=%fused_computation | loop fusion | flops 18874368 | bytes 18874368 | tf_op jit(solution)/shard_map/concatenate | solution.py:904
  278.1 0.0 copy-start.4
  278.1 0.0 copy-start.3
  278.1 0.0 copy-start.2
  278.1 0.0 copy-start.1
  278.1 0.0 copy-done
  278.1 2.5 convert_element_type.18
  280.6 0.0 copy-done.4
  280.6 0.7 copy.22
  281.3 0.0 copy-done.3
  281.3 0.8 copy.23
  282.1 0.0 copy-done.2
  282.1 0.8 copy.24
  282.9 0.0 copy-done.1
  282.9 0.8 copy.25
Async XLA Ops:
  272.9 5.2 %copy-start = (bf16[1024,1024]{1,0:T(8,128)(2,1)S(1)}, bf16[1024,1024]{1,0:T(8,128)(2,1)}, u32[]{:S(2)}) copy-start(bf16[1024,1024]{1,0:T(8,128)(2,1)} %get-tuple-element.19) | copy-start | bytes 6291460
  278.1 2.5 copy-start.4
  278.1 3.2 %copy-start.3 = (f32[128,1024]{1,0:T(8,128)S(1)}, f32[128,1024]{1,0:T(8,128)}, u32[]{:S(2)}) copy-start(f32[128,1024]{1,0:T(8,128)} %get-tuple-element.16) | copy-start | bytes 1572868
  278.1 4.0 %copy-start.2 = (f32[128,1024]{1,0:T(8,128)S(1)}, f32[128,1024]{1,0:T(8,128)}, u32[]{:S(2)}) copy-start(f32[128,1024]{1,0:T(8,128)} %get-tuple-element.41) | copy-start | bytes 1572868
  278.1 4.8 %copy-start.1 = (f32[128,1024]{1,0:T(8,128)S(1)}, f32[128,1024]{1,0:T(8,128)}, u32[]{:S(2)}) copy-start(f32[128,1024]{1,0:T(8,128)} %get-tuple-element.42) | copy-start | bytes 1572868

commit v2 on v1

--- a/solution.py
+++ b/solution.py
@@ -269,7 +269,7 @@
         self.recvs += count
         return base
 
-    def send(self, src, dst, slot, device):
+    def send(self, src, dst, slot, device, when=None):
         copy = pltpu.make_async_remote_copy(
             src_ref=src,
             dst_ref=dst,
@@ -279,13 +279,16 @@
             device_id_type=MESH,
         )
         self.sends += 1
-        copy.start()
-        self.pending.append(copy)
+        if when is None:
+            copy.start()
+        else:
+            pl.when(when)(copy.start)
+        self.pending.append((copy, when))
         return copy
 
     def sent(self, copy):
         copy.wait_send()
-        self.pending = [other for other in self.pending if other is not copy]
+        self.pending = [entry for entry in self.pending if entry[0] is not copy]
 
     def wait(self, dst, slot):
         pltpu.make_async_remote_copy(
@@ -298,11 +301,15 @@
         ).wait_recv()
 
     def drain(self):
-        for copy in self.pending:
-            copy.wait_send()
-
-
-SENDS, RECVS, LOCALS = 200, 200, 24
+        for copy, when in self.pending:
+            if when is None:
+                copy.wait_send()
+            else:
+                pl.when(when)(copy.wait_send)
+
+
+SENDS, RECVS, LOCALS = 256, 256, 24
+LEVELS = 4
 
 
 def scratch_of(rows, width, seqs, views, hidden):
@@ -311,6 +318,7 @@
     bf, f3 = jnp.bfloat16, jnp.float32
     vm = pltpu.VMEM
     mlp_rows = hidden * seqs * views // 4
+    half, quarter, eighth = width // 2, width // 4, width // 8
     return dict(
         w_full=vm((width, 3 * width), bf),
         w_own=vm((width, 3 * own), bf),
@@ -331,7 +339,7 @@
         middle=vm((rows, width), f3),
         normed_two=vm((4 * rows, width), bf),
         mixed_cot=vm((4 * rows, width), bf),
-        act_cot=vm((4 * rows, mlp_rows), f3),
+        slope=vm((4 * rows, mlp_rows), f3),
         act=vm((4 * rows, mlp_rows), bf),
         hid_cot=vm((4 * rows, mlp_rows), bf),
         part_own=vm((2, rows, width), f3),
@@ -340,8 +348,8 @@
         grad_keep=vm((2, mlp_rows // 2, width), bf),
         grad_pass=vm((2, mlp_rows // 2, width), bf),
         grad_core=vm((2, mlp_rows // 2, width), bf),
-        grad_in=vm((2, 4, hidden, width), bf),
-        branch=vm((length, width), bf),
+        grad_in=vm((2, LEVELS + 1, hidden, width), bf),
+        branch=vm((rows, width), bf),
         acot_tok=vm((rows, width), bf),
         acot=vm((length, own), bf),
         acot_s=vm((length, own), bf),
@@ -350,10 +358,17 @@
         pc_tok=vm((3, rows, width), bf),
         dw_out=vm((3, 3, width // seqs, own), bf),
         dw_in=vm((4, 3, width // seqs, own), bf),
-        do_out=vm((own, width), bf),
-        do_in=vm((4, own // seqs, width), bf),
-        fin_w=vm((3, width, width), bf),
-        fin_o=vm((width, width), bf),
+        dw_own=vm((3, width // seqs, own), bf),
+        do_keep=vm((half, width), f3),
+        do_core=vm((half, width), bf),
+        do_core_in=vm((half, width), bf),
+        do_y=vm((quarter, width), bf),
+        do_y_in=vm((quarter, width), bf),
+        do_x=vm((eighth, width), bf),
+        do_x_in=vm((eighth, width), bf),
+        do_z=vm((eighth, width), bf),
+        do_z_in=vm((LEVELS, eighth // LEVELS, width), bf),
+        do_own=vm((eighth // LEVELS, width), bf),
         gain_own=vm((8, width), f3),
         gain_in=vm((seqs, 8, width), f3),
         gain_sum=vm((8, width), f3),
@@ -374,7 +389,6 @@
     hidden = up_hbm.shape[0]
     mlp_rows = k.up.shape[0]
     half = mlp_rows // 2
-    levels = views // 2
     block = length // (SLOTS * SCENE_BLOCKS)
     scene = length // SLOTS
     scale = HEAD_DIM ** (-0.5)
@@ -385,33 +399,50 @@
     x, c, z, y = s // 2, s % 2, v // 2, v % 2
     x_s, c_s, xc_s = (1 - x) * 2 + c, x * 2 + (1 - c), (1 - x) * 2 + (1 - c)
     y_v = z * 2 + (1 - y)
-    others_z = [lax.rem(z + d, levels) for d in range(1, levels)]
+    z_pair, z_two, z_flip = z + 1 - 2 * (z % 2), lax.rem(z + 2, LEVELS), LEVELS - 1 - z
+    inner = (z == 1) | (z == 2)
+    outer = (z == 0) | (z == 3)
+    others_z = [z_pair, z_two, z_flip]
     group = [(x_s, v), (s, y_v), (x_s, y_v)]
     group_slot = [(1 - x) * 2 + y, x * 2 + (1 - y), (1 - x) * 2 + (1 - y)]
     own_slot = x * 2 + y
     view_peers = [lax.rem(v + d, views) for d in range(1, views)]
     seq_peers = [x_s, xc_s, c_s]
 
+    def level(zt):
+        return (s, zt * 2 + y)
+
     wires = Wires(k.send_sem, k.recv_sem, (c_s, v))
     in_normed = wires.inbox(views)
     in_ids = wires.inbox(views)
-    in_up = wires.inbox(levels + 1)
-    in_down = wires.inbox(levels + 1)
+    in_up = wires.inbox(LEVELS + 1)
+    in_down = wires.inbox(LEVELS + 1)
     in_mcot = wires.inbox(4)
     in_att = wires.inbox(views)
     in_two = wires.inbox(4)
     in_part = [wires.inbox(4), wires.inbox(4)]
     in_core = [wires.inbox(1), wires.inbox(1)]
-    in_grad = [wires.inbox(levels), wires.inbox(levels)]
+    in_grad = [wires.inbox(LEVELS + 1), wires.inbox(LEVELS + 1)]
     in_acot = wires.inbox(views)
-    in_branch = wires.inbox(views)
     in_pc = wires.inbox(views)
     in_dw = wires.inbox(seqs)
-    in_do = wires.inbox(seqs)
-    in_fw = wires.inbox(seqs * views)
-    in_fo = wires.inbox(seqs * views)
+    in_do = wires.inbox(3)
+    in_do_z = wires.inbox(LEVELS)
+    in_plane = wires.inbox(views)
+    in_query = wires.inbox(views)
+    in_cross = wires.inbox(views)
+    in_mate = [wires.inbox(views) for unused in range(3)]
+    in_out = wires.inbox(seqs * views)
     in_gain = wires.inbox(seqs)
     in_gains = wires.inbox(views)
+
+    def z_cast(src, dst, slot):
+        wires.send(src, dst, slot, level(z_pair))
+        wires.send(src, dst, slot, level(z_two))
+        wires.send(src, dst, slot, level(z_flip), when=inner)
+
+    def z_relay(ref, slot):
+        wires.send(ref, ref, slot, level(z_pair), when=inner)
 
     loads = []
 
@@ -421,7 +452,7 @@
         loads.append(copy)
         return copy
 
-    up_slot = at((c * levels + z) * hidden, hidden)
+    up_slot = at((c * LEVELS + z) * hidden, hidden)
     load_up = load(up_hbm, k.up.at[up_slot])
     load_down = load(down_hbm, k.down.at[up_slot])
     load_own = [
@@ -436,8 +467,8 @@
     for device in greeted:
         pl.semaphore_signal(barrier, inc=1, device_id=device, device_id_type=MESH)
 
-    gain_one = gain_one_ref[...].astype(f3)
-    gain_two = gain_two_ref[...].astype(f3)
+    gain_one = gain_one_ref[...].astype(f3).reshape(1, width)
+    gain_two = gain_two_ref[...].astype(f3).reshape(1, width)
     unit, _ = norm_stats(tok[...].astype(f3))
     k.normed[at(v * rows, rows), :] = (unit * gain_one).astype(bf)
     per = rows // block
@@ -456,16 +487,11 @@
 
     for p in view_peers:
         wires.send(k.ids_all.at[v], k.ids_all.at[v], in_ids + v, (s, p))
-    wires.send(view_rows(k.normed, v), view_rows(k.normed, v), in_normed + v, (s, y_v))
-    for zt in others_z:
-        wires.send(view_rows(k.normed, v), view_rows(k.normed, v), in_normed + v, (s, zt * 2 + y))
-
-    def send_mlp_rows(ref, base):
-        for zt in others_z:
-            wires.send(ref.at[up_slot], ref.at[up_slot], base + z, (s, zt * 2 + y))
-
+    mine = view_rows(k.normed, v)
+    wires.send(mine, mine, in_normed + v, (s, y_v))
+    z_cast(mine, mine, in_normed + v)
     load_up.wait()
-    send_mlp_rows(k.up, in_up)
+    z_cast(k.up.at[up_slot], k.up.at[up_slot], in_up + z)
 
     for p in view_peers:
         wires.wait(k.ids_all.at[p], in_ids + p)
@@ -495,8 +521,11 @@
     project(v)
     for zt in others_z:
         j = zt * 2 + y
-        wires.wait(view_rows(k.normed, j), in_normed + j)
-        wires.send(view_rows(k.normed, j), view_rows(k.normed, j), in_normed + j, (s, y_v))
+        there = view_rows(k.normed, j)
+        wires.wait(there, in_normed + j)
+        if zt is z_two:
+            z_relay(there, in_normed + j)
+        wires.send(there, there, in_normed + j, (s, y_v))
         project(j)
     for zt in [z] + others_z:
         j = zt * 2 + 1 - y
@@ -540,20 +569,25 @@
         wires.send(view_rows(k.att, p), k.att_tok.at[:, own_cols], in_att + v, (s, p))
     k.att_tok[:, own_cols] = k.att[at(v * rows, rows), :]
 
+    def mlp_slot(ref, zt):
+        return ref.at[at((c * LEVELS + zt) * hidden, hidden)]
+
+    def mlp_relay(ref, base):
+        wires.wait(mlp_slot(ref, z_two), base + z_two)
+        z_relay(mlp_slot(ref, z_two), base + z_two)
+
+    def core_exchange(ref, base):
+        for zt in (z_pair, z_flip):
+            wires.wait(mlp_slot(ref, zt), base + zt)
+        mine = ref.at[at(c * half, half)]
+        wires.send(mine, mine, base + LEVELS, (c_s, v))
+
+    mlp_relay(k.up, in_up)
     load_down.wait()
-    send_mlp_rows(k.down, in_down)
+    z_cast(k.down.at[up_slot], k.down.at[up_slot], in_down + z)
     mcot_own = at(own_slot * rows, rows)
     for device in group:
         wires.send(k.mixed_cot.at[mcot_own], k.mixed_cot.at[mcot_own], in_mcot + own_slot, device)
-
-    def core_exchange(ref, base):
-        for zt in others_z:
-            there = at((c * levels + zt) * hidden, hidden)
-            wires.wait(ref.at[there], base + zt)
-        mine = at(c * half, half)
-        wires.send(ref.at[mine], ref.at[mine], base + levels, (c_s, v))
-
-    core_exchange(k.up, in_up)
 
     load_wo.wait()
     for p in view_peers:
@@ -567,35 +601,45 @@
     for device in group:
         wires.send(k.normed_two.at[mcot_own], k.normed_two.at[mcot_own], in_two + own_slot, device)
 
-    for slot in group_slot:
-        there = at(slot * rows, rows)
-        wires.wait(k.mixed_cot.at[there], in_mcot + slot)
-    core_exchange(k.down, in_down)
-    theirs = at((1 - c) * half, half)
-    wires.wait(k.up.at[theirs], in_up + levels)
-    wires.wait(k.down.at[theirs], in_down + levels)
-
-    def cot_tile(n, unused):
-        k.act_cot[:, at(n * tile, tile)] = dot_inner(k.mixed_cot[...], k.down[at(n * tile, tile), :])
-        return unused
-
-    lax.fori_loop(0, mlp_rows // tile, cot_tile, 0)
-
-    def mlp_tile(slot):
+    core_exchange(k.up, in_up)
+    wires.wait(k.up.at[at((1 - c) * half, half)], in_up + LEVELS)
+
+    def hidden_tiles(slot):
         here = at(slot * rows, rows)
 
         def step(n, unused):
             cols = at(n * tile, tile)
             pre = dot_inner(k.normed_two[here, :], k.up[cols, :])
             below = 0.5 + 0.5 * lax.erf(pre * (0.5**0.5))
-            slope = below + pre * (jnp.exp(-0.5 * pre * pre) * (0.5 / math.pi) ** 0.5)
             k.act[here, cols] = (pre * below).astype(bf)
-            k.hid_cot[here, cols] = (k.act_cot[here, cols] * slope).astype(bf)
+            k.slope[here, cols] = below + pre * (jnp.exp(-0.5 * pre * pre) * (0.5 / math.pi) ** 0.5)
             return unused
 
         lax.fori_loop(0, mlp_rows // tile, step, 0)
 
-    def part_tiles(which, left, right, slot, dst):
+    hidden_tiles(own_slot)
+    mlp_relay(k.down, in_down)
+    for slot in group_slot:
+        wires.wait(k.normed_two.at[at(slot * rows, rows)], in_two + slot)
+        hidden_tiles(slot)
+
+    core_exchange(k.down, in_down)
+    wires.wait(k.down.at[at((1 - c) * half, half)], in_down + LEVELS)
+    for slot in group_slot:
+        wires.wait(k.mixed_cot.at[at(slot * rows, rows)], in_mcot + slot)
+
+    def cot_tiles(slot):
+        here = at(slot * rows, rows)
+
+        def step(n, unused):
+            cols = at(n * tile, tile)
+            up_to = dot_inner(k.mixed_cot[here, :], k.down[cols, :])
+            k.hid_cot[here, cols] = (up_to * k.slope[here, cols]).astype(bf)
+            return unused
+
+        lax.fori_loop(0, mlp_rows // tile, step, 0)
+
+    def part_tiles(left, right, slot, dst):
         here = at(slot * rows, rows)
 
         def step(n, unused):
@@ -605,13 +649,12 @@
 
         lax.fori_loop(0, width // tile, step, 0)
 
-    mlp_tile(own_slot)
-    for i, (slot, device) in enumerate(zip(group_slot, group)):
-        wires.wait(k.normed_two.at[at(slot * rows, rows)], in_two + slot)
-        mlp_tile(slot)
-        part_tiles(0, k.hid_cot, k.up, slot, k.part_out.at[0, i])
-        wires.send(k.part_out.at[0, i], k.part_in.at[0, own_slot], in_part[0] + own_slot, device)
-    part_tiles(0, k.hid_cot, k.up, own_slot, k.part_own.at[0])
+    for i in (2, 0, 1):
+        cot_tiles(group_slot[i])
+        part_tiles(k.hid_cot, k.up, group_slot[i], k.part_out.at[0, i])
+        wires.send(k.part_out.at[0, i], k.part_in.at[0, own_slot], in_part[0] + own_slot, group[i])
+    cot_tiles(own_slot)
+    part_tiles(k.hid_cot, k.up, own_slot, k.part_own.at[0])
 
     def grad_tiles(left, right, start, dst):
         def step(n, unused):
@@ -626,8 +669,54 @@
     for which, (left, right) in enumerate(pairs):
         grad_tiles(left, right, (1 - c) * half, k.grad_pass.at[which])
         passed.append(wires.send(k.grad_pass.at[which], k.grad_core.at[which], in_core[which], (c_s, v)))
-    for which, (left, right) in enumerate(pairs):
         grad_tiles(left, right, c * half, k.grad_keep.at[which])
+
+    def grad_level(which, zt):
+        there = at(zt * hidden, hidden)
+        return k.grad_keep[which, there, :].astype(f3) + k.grad_core[which, there, :].astype(f3)
+
+    def grad_piece(which, zt):
+        return k.grad_pass.at[which, at(zt * hidden, hidden)]
+
+    def add_cores(which):
+        wires.wait(k.grad_core.at[which], in_core[which])
+        wires.sent(passed[which])
+        for zt in others_z:
+            k.grad_pass[which, at(zt * hidden, hidden), :] = grad_level(which, zt).astype(bf)
+
+    def send_near(which):
+        wires.send(grad_piece(which, z_pair), k.grad_in.at[which, z], in_grad[which] + z, level(z_pair))
+
+    def send_far(which):
+        via = LEVELS
+        wires.send(grad_piece(which, z_two), k.grad_in.at[which, z], in_grad[which] + z, level(z_two), when=outer)
+        wires.send(grad_piece(which, z_flip), k.grad_in.at[which, via], in_grad[which] + via, level(z_pair), when=outer)
+        wires.send(grad_piece(which, z_flip), k.grad_in.at[which, z], in_grad[which] + z, level(z_flip), when=inner)
+
+    def send_joined(which):
+        @pl.when(inner)
+        def _():
+            wires.wait(k.grad_in.at[which, LEVELS], in_grad[which] + LEVELS)
+            there = at(z_two * hidden, hidden)
+            joined = k.grad_pass[which, there, :].astype(f3) + k.grad_in[which, LEVELS].astype(f3)
+            k.grad_pass[which, there, :] = joined.astype(bf)
+
+        wires.send(grad_piece(which, z_two), k.grad_in.at[which, z], in_grad[which] + z, level(z_two), when=inner)
+
+    def collect(which, dst):
+        total = grad_level(which, z)
+        for zt in (z_pair, z_two):
+            wires.wait(k.grad_in.at[which, zt], in_grad[which] + zt)
+            total = total + k.grad_in[which, zt].astype(f3)
+        dst[...] = total
+
+        @pl.when(inner)
+        def _():
+            wires.wait(k.grad_in.at[which, z_flip], in_grad[which] + z_flip)
+            dst[...] = dst[...] + k.grad_in[which, z_flip].astype(f3)
+
+    add_cores(0)
+    send_near(0)
 
     def part_sum(which):
         total = k.part_own[which]
@@ -641,43 +730,39 @@
     k.gain_own[1:2, :] = jnp.sum(cot_two * unit_two, axis=0, keepdims=True)
     middle_cot = out_cot[...].astype(f3) + norm_back(cot_two, unit_two, inverse_two, gain_two)
     tokens_grad[...] = middle_cot
-    k.branch[at(v * rows, rows), :] = (live * middle_cot).astype(bf)
+    k.branch[...] = (live * middle_cot).astype(bf)
     for n in range(width // tile):
         k.acot_tok[:, pl.ds(n * tile, tile)] = dot_inner(
-            k.branch[at(v * rows, rows), :], k.wo[pl.ds(n * tile, tile), :]
+            k.branch[...], k.wo[pl.ds(n * tile, tile), :]
         ).astype(bf)
     for p in view_peers:
         wires.send(k.acot_tok.at[:, at(p * own, own)], view_rows(k.acot, v), in_acot + v, (s, p))
     k.acot[at(v * rows, rows), :] = k.acot_tok[:, own_cols]
-    wires.send(view_rows(k.branch, v), view_rows(k.branch, v), in_branch + v, (s, y_v))
-    for zt in others_z:
-        wires.send(view_rows(k.branch, v), view_rows(k.branch, v), in_branch + v, (s, zt * 2 + y))
-
-    def grad_level(which, zt):
-        there = at(zt * hidden, hidden)
-        return k.grad_keep[which, there, :].astype(f3) + k.grad_core[which, there, :].astype(f3)
-
-    for which in range(2):
-        wires.wait(k.grad_core.at[which], in_core[which])
-        wires.sent(passed[which])
-        for zt in others_z:
-            k.grad_pass[which, at(zt * hidden, hidden), :] = grad_level(which, zt).astype(bf)
-
-    def send_grads(which):
-        for zt in others_z:
-            wires.send(
-                k.grad_pass.at[which, at(zt * hidden, hidden)],
-                k.grad_in.at[which, z],
-                in_grad[which] + z,
-                (s, zt * 2 + y),
-            )
-
-    send_grads(0)
-
-    for i, (slot, device) in enumerate(zip(group_slot, group)):
-        part_tiles(1, k.act, k.down, slot, k.part_out.at[1, i])
-        wires.send(k.part_out.at[1, i], k.part_in.at[1, own_slot], in_part[1] + own_slot, device)
-    part_tiles(1, k.act, k.down, own_slot, k.part_own.at[1])
+    send_far(0)
+
+    o_half, o_quarter, o_eighth = width // 2, width // 4, width // 8
+    o_piece = o_eighth // LEVELS
+
+    def outer_rows(start, dst, dtype):
+        def step(n, unused):
+            there = at(n * tile, tile)
+            left = k.att_tok[:, at(start + n * tile, tile)]
+            dst[there, :] = dot_outer(left, k.branch[...]).astype(dtype)
+            return unused
+
+        lax.fori_loop(0, o_half // tile, step, 0)
+
+    outer_rows((1 - c) * o_half, k.do_core, bf)
+    wires.send(k.do_core, k.do_core_in, in_do, (c_s, v))
+    outer_rows(c * o_half, k.do_keep, f3)
+    for i in (2, 0, 1):
+        part_tiles(k.act, k.down, group_slot[i], k.part_out.at[1, i])
+        wires.send(k.part_out.at[1, i], k.part_in.at[1, own_slot], in_part[1] + own_slot, group[i])
+    part_tiles(k.act, k.down, own_slot, k.part_own.at[1])
+    wires.wait(k.do_core_in, in_do)
+    k.do_keep[...] = k.do_keep[...] + k.do_core_in[...].astype(f3)
+    k.do_y[...] = k.do_keep[at((1 - y) * o_quarter, o_quarter), :].astype(bf)
+    wires.send(k.do_y, k.do_y_in, in_do + 1, (s, y_v))
 
     for p in view_peers:
         wires.wait(view_rows(k.acot, p), in_acot + p)
@@ -709,7 +794,6 @@
         return unused
 
     lax.fori_loop(0, SLOTS, attend_back, 0)
-
     pc_blocks = k.pc_s.reshape(count, block, 3 * own)
 
     def unsort(i, unused):
@@ -723,63 +807,65 @@
         wires.send(k.pc.at[:, at(p * rows, rows)], k.pc_tok.at[:, :, own_cols], in_pc + v, (s, p))
     for t in range(3):
         k.pc_tok[t, :, own_cols] = k.pc[t, at(v * rows, rows), :]
-    send_grads(1)
-
-    for zt in others_z:
-        j = zt * 2 + y
-        wires.wait(view_rows(k.branch, j), in_branch + j)
-        wires.send(view_rows(k.branch, j), view_rows(k.branch, j), in_branch + j, (s, y_v))
 
     part = width // seqs
     for i, p in enumerate(seq_peers):
         for t in range(3):
             k.dw_out[i, t] = dot_outer(k.normed[:, at(p * part, part)], k.pc[t]).astype(bf)
         wires.send(k.dw_out.at[i], k.dw_in.at[s], in_dw + s, (p, v))
-    for zt in [z] + others_z:
-        j = zt * 2 + 1 - y
-        wires.wait(view_rows(k.branch, j), in_branch + j)
-    for n in range(width // tile):
-        cols = pl.ds(n * tile, tile)
-        k.do_out[:, cols] = dot_outer(k.att[...], k.branch[:, cols]).astype(bf)
-    piece = own // seqs
-    for p in seq_peers:
-        wires.send(k.do_out.at[at(p * piece, piece)], k.do_in.at[s], in_do + s, (p, v))
     own_part = at(s * part, part)
     own_dw = [dot_outer(k.normed[:, own_part], k.pc[t]) for t in range(3)]
+    send_joined(0)
+    wires.wait(k.do_y_in, in_do + 1)
+    o_mine = at(y * o_quarter, o_quarter)
+    k.do_keep[o_mine, :] = k.do_keep[o_mine, :] + k.do_y_in[...].astype(f3)
+    k.do_x[...] = k.do_keep[at(y * o_quarter + (1 - x) * o_eighth, o_eighth), :].astype(bf)
+    wires.send(k.do_x, k.do_x_in, in_do + 2, (x_s, v))
     for p in seq_peers:
         wires.wait(k.dw_in.at[p], in_dw + p)
     for t in range(3):
         total = own_dw[t]
         for p in seq_peers:
             total = total + k.dw_in[p, t].astype(f3)
-        k.fin_w[t, own_part, own_cols] = total.astype(bf)
-    for p in seq_peers:
-        wires.wait(k.do_in.at[p], in_do + p)
-    total = k.do_out[at(s * piece, piece), :].astype(f3)
-    for p in seq_peers:
-        total = total + k.do_in[p].astype(f3)
-
-    def fin_w(q, j):
-        return k.fin_w.at[:, at(q * part, part), at(j * own, own)]
-
-    def fin_o(q, j):
-        return k.fin_o.at[at(j * own + q * piece, piece)]
-
-    k.fin_o[at(v * own + s * piece, piece), :] = total.astype(bf)
-
-    def pass_on(q, j, device):
-        wires.send(fin_w(q, j), fin_w(q, j), in_fw + q * views + j, device)
-        wires.send(fin_o(q, j), fin_o(q, j), in_fo + q * views + j, device)
-
-    def arrive(q, j):
-        wires.wait(fin_w(q, j), in_fw + q * views + j)
-        wires.wait(fin_o(q, j), in_fo + q * views + j)
-
-    pass_on(s, v, (s, y_v))
+        k.dw_own[t] = total.astype(bf)
+
+    def w_at(q, j, first, last):
+        return w_grad.at[pl.ds(first, last - first), at(q * part, part), at(j * own, own)]
+
+    def w_plane(j):
+        return w_at(s, j, 0, 3)
+
+    def w_query(j):
+        return w_at(x_s, j, 0, 1)
+
+    def w_cross(q, j):
+        return w_at(q, j, 1, 3)
+
+    wires.send(k.dw_own.at[pl.ds(0, 1)], w_at(s, v, 0, 1), in_query + v, (x_s, v))
+    wires.send(k.dw_own, w_plane(v), in_plane + v, (s, y_v))
+    z_cast(k.dw_own, w_plane(v), in_plane + v)
+    wires.send(k.dw_own.at[pl.ds(1, 2)], w_cross(s, v), in_cross + v, (x_s, v))
+    wires.send(k.dw_own, w_plane(v), in_mate[0] + v, (c_s, v))
+    keep_w = load(k.dw_own, w_plane(v))
+
+    wires.wait(w_query(v), in_query + v)
+    wires.send(w_query(v), w_query(v), in_query + v, (s, y_v))
+    z_cast(w_query(v), w_query(v), in_query + v)
+    wires.send(w_query(v), w_query(v), in_mate[1] + v, (c_s, v))
+
+    wires.wait(k.do_x_in, in_do + 2)
+    total = k.do_keep[at(y * o_quarter + x * o_eighth, o_eighth), :] + k.do_x_in[...].astype(f3)
+    k.do_z[...] = total.astype(bf)
+
+    def o_level(zt):
+        return at(zt * o_piece, o_piece)
+
     for zt in others_z:
-        pass_on(s, v, (s, zt * 2 + y))
-    pass_on(s, v, (x_s, v))
-    pass_on(s, v, (c_s, v))
+        wires.send(k.do_z.at[o_level(zt)], k.do_z_in.at[z], in_do_z + z, level(zt))
+
+    add_cores(1)
+    send_near(1)
+    send_far(1)
 
     load_w.wait()
     for p in view_peers:
@@ -802,16 +888,54 @@
     for p in seq_peers:
         wires.send(k.gain_own, k.gain_in.at[s], in_gain + s, (p, v))
 
+    def o_at(q, j):
+        at_c, at_x, at_y, at_z = q % 2, q // 2, j % 2, j // 2
+        return o_grad.at[at(at_c * o_half + at_y * o_quarter + at_x * o_eighth + at_z * o_piece, o_piece)]
+
+    def to_mate(which, ref, j):
+        wires.send(ref, ref, in_mate[which] + j, (c_s, v))
+
+    def pass_plane(zt, row_y):
+        j = zt * 2 + row_y
+        wires.wait(w_plane(j), in_plane + j)
+        if row_y is y:
+            if zt is z_two:
+                z_relay(w_plane(j), in_plane + j)
+            wires.send(w_plane(j), w_plane(j), in_plane + j, (s, y_v))
+        wires.send(w_cross(s, j), w_cross(s, j), in_cross + j, (x_s, v))
+        to_mate(0, w_plane(j), j)
+
+    def pass_query(zt, row_y):
+        j = zt * 2 + row_y
+        wires.wait(w_query(j), in_query + j)
+        if row_y is y:
+            if zt is z_two:
+                z_relay(w_query(j), in_query + j)
+            wires.send(w_query(j), w_query(j), in_query + j, (s, y_v))
+        to_mate(1, w_query(j), j)
+
+    across = 1 - y
     for zt in others_z:
-        j = zt * 2 + y
-        arrive(s, j)
-        for device in ((s, y_v), (x_s, v), (c_s, v)):
-            pass_on(s, j, device)
+        pass_plane(zt, y)
+    pass_plane(z, across)
+    total = k.do_keep[at(y * o_quarter + x * o_eighth + z * o_piece, o_piece), :]
+    total = total + k.do_x_in[o_level(z), :].astype(f3)
+    for zt in others_z:
+        wires.wait(k.do_z_in.at[zt], in_do_z + zt)
+        total = total + k.do_z_in[zt].astype(f3)
+    k.do_own[...] = total.astype(bf)
+    wires.send(k.do_own, o_at(s, v), in_out + s * views + v, (s, y_v))
+    z_cast(k.do_own, o_at(s, v), in_out + s * views + v)
+    wires.send(k.do_own, o_at(s, v), in_out + s * views + v, (x_s, v))
+    wires.send(k.do_own, o_at(s, v), in_out + s * views + v, (c_s, v))
+    keep_o = load(k.do_own, o_at(s, v))
+    for zt in others_z:
+        pass_query(zt, y)
+    send_joined(1)
+    for zt in others_z:
+        pass_plane(zt, across)
     for zt in [z] + others_z:
-        j = zt * 2 + 1 - y
-        arrive(s, j)
-        for device in ((x_s, v), (c_s, v)):
-            pass_on(s, j, device)
+        pass_query(zt, across)
 
     total = k.gain_own[...]
     for p in seq_peers:
@@ -821,13 +945,28 @@
     for p in view_peers:
         wires.send(k.gain_sum, k.gain_all.at[v], in_gains + v, (s, p))
 
+    def pass_out(q, j, devices, relay):
+        slot = in_out + q * views + j
+        wires.wait(o_at(q, j), slot)
+        if relay:
+            z_relay(o_at(q, j), slot)
+        for device in devices:
+            wires.send(o_at(q, j), o_at(q, j), slot, device)
+
+    for zt in others_z:
+        pass_out(s, zt * 2 + y, [(s, y_v), (x_s, v), (c_s, v)], zt is z_two)
+    for zt in [z] + others_z:
+        pass_out(s, zt * 2 + across, [(x_s, v), (c_s, v)], False)
+
     layer_out[...] = (k.middle[...] + live * part_sum(1)).astype(bf)
-    for which, dst in enumerate((down_grad, up_grad)):
-        total = grad_level(which, z)
-        for zt in others_z:
-            wires.wait(k.grad_in.at[which, zt], in_grad[which] + zt)
-            total = total + k.grad_in[which, zt].astype(f3)
-        dst[...] = total
+    collect(0, down_grad)
+    by_arrival = [v] + [zt * 2 + y for zt in others_z] + [zt * 2 + across for zt in [z] + others_z]
+    for j in by_arrival:
+        wires.wait(w_cross(x_s, j), in_cross + j)
+        to_mate(2, w_cross(x_s, j), j)
+    for j in by_arrival:
+        pass_out(x_s, j, [(c_s, v)], False)
+    collect(1, up_grad)
 
     total = k.gain_sum[...]
     for p in view_peers:
@@ -835,19 +974,30 @@
         total = total + k.gain_all[p]
     gains[...] = total
 
-    for j in [v, y_v] + [p for zt in others_z for p in (zt * 2 + y, zt * 2 + 1 - y)]:
-        arrive(x_s, j)
-        pass_on(x_s, j, (c_s, v))
     for j in range(views):
-        arrive(c_s, j)
-        arrive(xc_s, j)
-    out_w = pltpu.make_async_copy(k.fin_w, w_grad, k.local_sem.at[LOCALS - 1])
-    out_o = pltpu.make_async_copy(k.fin_o, o_grad, k.local_sem.at[LOCALS - 2])
-    out_w.start()
-    out_o.start()
+        wires.wait(w_at(c_s, j, 0, 3), in_mate[0] + j)
+        wires.wait(w_at(xc_s, j, 0, 1), in_mate[1] + j)
+        wires.wait(w_cross(xc_s, j), in_mate[2] + j)
+        for q in (c_s, xc_s):
+            wires.wait(o_at(q, j), in_out + q * views + j)
+    keep_w.wait()
+    keep_o.wait()
     wires.drain()
-    out_w.wait()
-    out_o.wait()
+
+
+def finish_kernel(*refs):
+    (layer_in, tokens_in, gains, w_in, o_in, up_in, down_in) = refs[:7]
+    (layer_out, tokens_grad, gain_one, w_out, o_out, gain_two, up_out, down_out) = refs[7:]
+    width = w_in.shape[2]
+    for t in range(3):
+        w_out[:, t * width : (t + 1) * width] = w_in[t].astype(jnp.float32)
+    o_out[...] = o_in[...].astype(jnp.float32)
+    layer_out[...] = layer_in[...]
+    tokens_grad[...] = tokens_in[...]
+    up_out[...] = up_in[...]
+    down_out[...] = down_in[...]
+    gain_one[...] = gains[0:1, :].reshape(width)
+    gain_two[...] = gains[1:2, :].reshape(width)
 
 
 def fused(
@@ -871,7 +1021,7 @@
     anywhere = pl.BlockSpec(memory_space=pl.ANY)
     shape = jax.ShapeDtypeStruct
     bf, f3 = jnp.bfloat16, jnp.float32
-    layer_out, tokens_grad, gains, w_grad, o_grad, up_grad, down_grad = pl.pallas_call(
+    parts = pl.pallas_call(
         functools.partial(layer_kernel, tuple(spec), seqs, views),
         out_shape=(
             shape((rows, width), bf),
@@ -894,21 +1044,47 @@
         scene_ids,
         live_mask,
         out_grad[0],
-        attention_gain[None],
-        feedforward_gain[None],
+        attention_gain,
+        feedforward_gain,
         input_weight,
         output_weight,
         up_weight,
         down_weight,
     )
-    wide = jnp.concatenate([w_grad[t].astype(f3) for t in range(3)], axis=1)
+    steps = 8
+
+    def slab(*lead):
+        full = lead + (width,)
+        block = full[:-2] + (full[-2] // steps, width)
+        return pl.BlockSpec(block, lambda i: (0,) * (len(block) - 2) + (i, 0))
+
+    whole = pl.BlockSpec((8, width), lambda i: (0, 0))
+    line = pl.BlockSpec((width,), lambda i: (0,))
+    thick = pl.BlockSpec((width // steps, 3 * width), lambda i: (i, 0))
+    layer_out, tokens_grad, gain_one, w_grad, o_grad, gain_two, up_grad, down_grad = pl.pallas_call(
+        finish_kernel,
+        grid=(steps,),
+        out_shape=(
+            shape((rows, width), bf),
+            shape((rows, width), f3),
+            shape((width,), f3),
+            shape((width, 3 * width), f3),
+            shape((width, width), f3),
+            shape((width,), f3),
+            shape((hidden, width), f3),
+            shape((hidden, width), f3),
+        ),
+        in_specs=[slab(rows), slab(rows), whole, slab(3, width), slab(width), slab(hidden), slab(hidden)],
+        out_specs=(slab(rows), slab(rows), line, thick, slab(width), line, slab(hidden), slab(hidden)),
+        name="finish",
+    )(*parts)
     return (
         layer_out[None],
         tokens_grad[None],
-        gains[0],
-        wide,
-        o_grad.astype(f3),
-        gains[1],
+        gain_one,
+        w_grad,
+        o_grad,
+        gain_two,
         up_grad,
         down_grad,
     )
@@ -916,7 +1092,7 @@
 
 def solution(mesh):
     seqs, views = mesh.shape["seq"], mesh.shape["view"]
-    small = seqs == 4 and views % 2 == 0 and HEADS == 2 * views
+    small = seqs == 4 and views == 2 * LEVELS and HEADS == 2 * views
     body = functools.partial(fused, seqs, views) if small else shards
     return jax.shard_map(
         body,

time: 284 us -> 204 us (0.72)
  the two profiles are of different devices: /device:TPU:13 before, /device:TPU:0 now
where the time goes in v2:
time: 204 us
  Pallas kernels  203 us (100%)
    pallas_call x1, Pallas kernels, fused(): pl.pallas_call(functools.partial(layer_kernel, tuple(spec), seqs, views),...  192 us
    pallas_call x1, Pallas kernels, fused(): pl.pallas_call(finish_kernel, grid=(steps,), out_shape=(shape((rows, widt...  11.1 us

profile of v2, /device:TPU:0, one launch (start us, length us, event | category | flops | bytes accessed | tf_op | source)
XLA Modules:
  0.0 203.5 jit_solution(13227502330951194837)
XLA Ops:
  0.6 191.6 %layer.1 = (bf16[128,1024]{1,0:T(8,128)(2,1)}, f32[128,1024]{1,0:T(8,128)}, f32[8,1024]{1,0:T(8,128)}, bf16[3,1024,1024]{2,1,0:T(8,128)(2,1)}, bf16[1024,1024]{1...) custom-call(bf16[128,1024]{1,0:T(8,128)(2,1)} %bitcast.4, s32[1,128]{1,0:T(1,128)} %refs_1_.1, ...), custom_call_target="tpu_custom_call" | custom-call | tf_op jit(solution)/shard_map/layer/pallas_call | solution.py:1024
  192.3 11.1 %finish.1 = (bf16[128,1024]{1,0:T(8,128)(2,1)}, f32[128,1024]{1,0:T(8,128)}, f32[1024]{0:T(1024)}, f32[1024,3072]{1,0:T(8,128)}, f32[1024,1024]{1,0:T(8,128)}, /...) custom-call(bf16[128,1024]{1,0:T(8,128)(2,1)} %get-tuple-element.23.refs_0_, ...), custom_call_target="tpu_custom_call" | custom-call | tf_op jit(solution)/shard_map/finish/pallas_call | solution.py:1064

commit v3 on v2

--- a/solution.py
+++ b/solution.py
@@ -262,53 +262,65 @@
 class Wires:
     def __init__(self, send_sem, recv_sem, peer):
         self.send_sem, self.recv_sem, self.peer = send_sem, recv_sem, peer
-        self.sends, self.recvs, self.pending = 0, 0, []
+        self.free, self.recvs, self.total, self.pending = list(range(SENDS)), 0, 0, []
 
     def inbox(self, count):
         base = self.recvs
         self.recvs += count
+        assert self.recvs <= RECVS
         return base
 
-    def send(self, src, dst, slot, device, when=None):
-        copy = pltpu.make_async_remote_copy(
+    def bulk(self):
+        return self.free.pop(0)
+
+    def copy(self, src, dst, lane, slot, device):
+        return pltpu.make_async_remote_copy(
             src_ref=src,
             dst_ref=dst,
-            send_sem=self.send_sem.at[self.sends],
+            send_sem=self.send_sem.at[lane],
             recv_sem=self.recv_sem.at[slot],
             device_id=device,
             device_id_type=MESH,
         )
-        self.sends += 1
+
+    def send(self, src, dst, slot, device, when=None, bulk=None):
+        lane = self.free.pop(0) if bulk is None else bulk
+        copy = self.copy(src, dst, lane, slot, device)
         if when is None:
             copy.start()
         else:
             pl.when(when)(copy.start)
-        self.pending.append((copy, when))
+        if bulk is None:
+            self.pending.append((self.total, copy, when, lane))
+            self.total += 1
         return copy
 
+    def finish(self, entry):
+        unused, copy, when, lane = entry
+        if when is None:
+            copy.wait_send()
+        else:
+            pl.when(when)(copy.wait_send)
+        self.free.append(lane)
+
     def sent(self, copy):
-        copy.wait_send()
-        self.pending = [entry for entry in self.pending if entry[0] is not copy]
+        for entry in [entry for entry in self.pending if entry[1] is copy]:
+            self.finish(entry)
+        self.pending = [entry for entry in self.pending if entry[1] is not copy]
+
+    def settle(self, until):
+        for entry in [entry for entry in self.pending if entry[0] < until]:
+            self.finish(entry)
+        self.pending = [entry for entry in self.pending if entry[0] >= until]
+
+    def settle_bulk(self, whole, lane):
+        self.copy(whole, whole, lane, 0, self.peer).wait_send()
 
     def wait(self, dst, slot):
-        pltpu.make_async_remote_copy(
-            src_ref=dst,
-            dst_ref=dst,
-            send_sem=self.send_sem.at[0],
-            recv_sem=self.recv_sem.at[slot],
-            device_id=self.peer,
-            device_id_type=MESH,
-        ).wait_recv()
-
-    def drain(self):
-        for copy, when in self.pending:
-            if when is None:
-                copy.wait_send()
-            else:
-                pl.when(when)(copy.wait_send)
-
-
-SENDS, RECVS, LOCALS = 256, 256, 24
+        self.copy(dst, dst, 0, slot, self.peer).wait_recv()
+
+
+SENDS, RECVS, LOCALS = 80, 124, 16
 LEVELS = 4
 
 
@@ -320,6 +332,12 @@
     mlp_rows = hidden * seqs * views // 4
     half, quarter, eighth = width // 2, width // 4, width // 8
     return dict(
+        tok=vm((rows, width), bf),
+        out_cot=vm((rows, width), bf),
+        layer_out=vm((rows, width), bf),
+        tokens_grad=vm((rows, width), f3),
+        up_grad=vm((hidden, width), f3),
+        down_grad=vm((hidden, width), f3),
         w_full=vm((width, 3 * width), bf),
         w_own=vm((width, 3 * own), bf),
         wo=vm((width, width), bf),
@@ -340,6 +358,7 @@
         normed_two=vm((4 * rows, width), bf),
         mixed_cot=vm((4 * rows, width), bf),
         slope=vm((4 * rows, mlp_rows), f3),
+        part_all=vm((4 * rows, width), f3),
         act=vm((4 * rows, mlp_rows), bf),
         hid_cot=vm((4 * rows, mlp_rows), bf),
         part_own=vm((2, rows, width), f3),
@@ -356,8 +375,9 @@
         pc_s=vm((length, 3 * own), bf),
         pc=vm((3, length, own), bf),
         pc_tok=vm((3, rows, width), bf),
-        dw_out=vm((3, 3, width // seqs, own), bf),
-        dw_in=vm((4, 3, width // seqs, own), bf),
+        dw_out=vm((2, 3, width // seqs, own), bf),
+        dw_x=vm((3, width // seqs, own), bf),
+        dw_in=vm((3, 3, width // seqs, own), bf),
         dw_own=vm((3, width // seqs, own), bf),
         do_keep=vm((half, width), f3),
         do_core=vm((half, width), bf),
@@ -380,9 +400,11 @@
 
 
 def layer_kernel(names, seqs, views, *refs):
-    (tok, ids, alive, out_cot, gain_one_ref, gain_two_ref, w_hbm, wo_hbm, up_hbm, down_hbm) = refs[:10]
-    (layer_out, tokens_grad, gains, w_grad, o_grad, up_grad, down_grad) = refs[10:17]
+    (tok_hbm, ids, alive, cot_hbm, gain_one_ref, gain_two_ref, w_hbm, wo_hbm, up_hbm, down_hbm) = refs[:10]
+    (layer_hbm, tokens_hbm, gains, w_grad, o_grad, up_hbm_out, down_hbm_out) = refs[10:17]
     k = types.SimpleNamespace(**dict(zip(names, refs[17:])))
+    tok, out_cot = k.tok, k.out_cot
+    layer_out, tokens_grad, up_grad, down_grad = k.layer_out, k.tokens_grad, k.up_grad, k.down_grad
     rows, width = tok.shape
     length = rows * views
     own = width // views
@@ -423,18 +445,21 @@
     in_part = [wires.inbox(4), wires.inbox(4)]
     in_core = [wires.inbox(1), wires.inbox(1)]
     in_grad = [wires.inbox(LEVELS + 1), wires.inbox(LEVELS + 1)]
-    in_acot = wires.inbox(views)
-    in_pc = wires.inbox(views)
-    in_dw = wires.inbox(seqs)
+    in_acot, in_pc = in_ids, in_att
+    in_dw = wires.inbox(3)
     in_do = wires.inbox(3)
     in_do_z = wires.inbox(LEVELS)
     in_plane = wires.inbox(views)
     in_query = wires.inbox(views)
     in_cross = wires.inbox(views)
-    in_mate = [wires.inbox(views) for unused in range(3)]
-    in_out = wires.inbox(seqs * views)
+    in_mate = [wires.inbox(1) for unused in range(3)]
+    in_out = [wires.inbox(views), wires.inbox(views)]
+    in_out_mate = wires.inbox(1)
     in_gain = wires.inbox(seqs)
-    in_gains = wires.inbox(views)
+    in_gains = in_normed
+    to_view = [wires.bulk() for unused in range(5)]
+    to_mate_w = [wires.bulk() for unused in range(3)]
+    to_mate_o = wires.bulk()
 
     def z_cast(src, dst, slot):
         wires.send(src, dst, slot, level(z_pair))
@@ -444,7 +469,12 @@
     def z_relay(ref, slot):
         wires.send(ref, ref, slot, level(z_pair), when=inner)
 
-    loads = []
+    barrier = pltpu.get_barrier_semaphore()
+    greeted = [(s, p) for p in view_peers] + [(p, v) for p in seq_peers] + [(x_s, y_v)]
+    for device in greeted:
+        pl.semaphore_signal(barrier, inc=1, device_id=device, device_id_type=MESH)
+
+    loads, kept = [], []
 
     def load(src, dst):
         copy = pltpu.make_async_copy(src, dst, k.local_sem.at[len(loads)])
@@ -453,6 +483,8 @@
         return copy
 
     up_slot = at((c * LEVELS + z) * hidden, hidden)
+    load_tok = load(tok_hbm, tok)
+    load_cot = load(cot_hbm, out_cot)
     load_up = load(up_hbm, k.up.at[up_slot])
     load_down = load(down_hbm, k.down.at[up_slot])
     load_own = [
@@ -462,13 +494,9 @@
     load_wo = load(wo_hbm, k.wo)
     load_w = load(w_hbm, k.w_full)
 
-    barrier = pltpu.get_barrier_semaphore()
-    greeted = [(s, p) for p in view_peers] + [(p, v) for p in seq_peers] + [(x_s, y_v)]
-    for device in greeted:
-        pl.semaphore_signal(barrier, inc=1, device_id=device, device_id_type=MESH)
-
     gain_one = gain_one_ref[...].astype(f3).reshape(1, width)
     gain_two = gain_two_ref[...].astype(f3).reshape(1, width)
+    load_tok.wait()
     unit, _ = norm_stats(tok[...].astype(f3))
     k.normed[at(v * rows, rows), :] = (unit * gain_one).astype(bf)
     per = rows // block
@@ -479,19 +507,24 @@
         scenes = jnp.where(lane == v * per + m, mine, scenes)
     k.ids_all[v] = jnp.broadcast_to(scenes, (8, 128))
     live = jnp.transpose(jnp.broadcast_to(alive[...].astype(f3), (rows, rows)))[:, :1]
-    k.mixed_cot[at(own_slot * rows, rows), :] = (live * out_cot[...].astype(f3)).astype(bf)
     pl.semaphore_wait(barrier, len(greeted))
 
     def view_rows(ref, j):
         return ref.at[at(j * rows, rows)]
 
     for p in view_peers:
-        wires.send(k.ids_all.at[v], k.ids_all.at[v], in_ids + v, (s, p))
+        wires.send(k.ids_all.at[v], k.ids_all.at[v], in_ids + v, (s, p), bulk=to_view[0])
     mine = view_rows(k.normed, v)
     wires.send(mine, mine, in_normed + v, (s, y_v))
     z_cast(mine, mine, in_normed + v)
-    load_up.wait()
-    z_cast(k.up.at[up_slot], k.up.at[up_slot], in_up + z)
+    load_cot.wait()
+    mcot_own = at(own_slot * rows, rows)
+    k.mixed_cot[mcot_own, :] = (live * out_cot[...].astype(f3)).astype(bf)
+
+    def send_mcot(device):
+        wires.send(k.mixed_cot.at[mcot_own], k.mixed_cot.at[mcot_own], in_mcot + own_slot, device)
+
+    send_mcot(group[0])
 
     for p in view_peers:
         wires.wait(k.ids_all.at[p], in_ids + p)
@@ -526,11 +559,37 @@
         if zt is z_two:
             z_relay(there, in_normed + j)
         wires.send(there, there, in_normed + j, (s, y_v))
+        if zt is z_two:
+            load_up.wait()
+            z_cast(k.up.at[up_slot], k.up.at[up_slot], in_up + z)
         project(j)
     for zt in [z] + others_z:
         j = zt * 2 + 1 - y
         wires.wait(view_rows(k.normed, j), in_normed + j)
         project(j)
+    def mlp_slot(ref, zt):
+        return ref.at[at((c * LEVELS + zt) * hidden, hidden)]
+
+    def mlp_relay(ref, base):
+        @pl.when(inner)
+        def _():
+            wires.wait(mlp_slot(ref, z_two), base + z_two)
+
+        z_relay(mlp_slot(ref, z_two), base + z_two)
+
+    def core_exchange(ref, base):
+        @pl.when(outer)
+        def _():
+            wires.wait(mlp_slot(ref, z_two), base + z_two)
+
+        for zt in (z_pair, z_flip):
+            wires.wait(mlp_slot(ref, zt), base + zt)
+        mine = ref.at[at(c * half, half)]
+        wires.send(mine, mine, base + LEVELS, (c_s, v))
+
+    mlp_relay(k.up, in_up)
+    send_mcot(group[1])
+    send_mcot(group[2])
     to_scalar.wait()
 
     def reorder(dst, src, row):
@@ -566,28 +625,9 @@
     reorder(k.att, k.att_s, 8)
     own_cols = at(v * own, own)
     for p in view_peers:
-        wires.send(view_rows(k.att, p), k.att_tok.at[:, own_cols], in_att + v, (s, p))
+        wires.send(view_rows(k.att, p), k.att_tok.at[:, own_cols], in_att + v, (s, p), bulk=to_view[1])
     k.att_tok[:, own_cols] = k.att[at(v * rows, rows), :]
 
-    def mlp_slot(ref, zt):
-        return ref.at[at((c * LEVELS + zt) * hidden, hidden)]
-
-    def mlp_relay(ref, base):
-        wires.wait(mlp_slot(ref, z_two), base + z_two)
-        z_relay(mlp_slot(ref, z_two), base + z_two)
-
-    def core_exchange(ref, base):
-        for zt in (z_pair, z_flip):
-            wires.wait(mlp_slot(ref, zt), base + zt)
-        mine = ref.at[at(c * half, half)]
-        wires.send(mine, mine, base + LEVELS, (c_s, v))
-
-    mlp_relay(k.up, in_up)
-    load_down.wait()
-    z_cast(k.down.at[up_slot], k.down.at[up_slot], in_down + z)
-    mcot_own = at(own_slot * rows, rows)
-    for device in group:
-        wires.send(k.mixed_cot.at[mcot_own], k.mixed_cot.at[mcot_own], in_mcot + own_slot, device)
 
     load_wo.wait()
     for p in view_peers:
@@ -598,8 +638,11 @@
         k.middle[:, cols] = tok[:, cols].astype(f3) + live * dot_nn(k.att_tok[...], k.wo[:, cols])
     unit_two, _ = norm_stats(k.middle[...])
     k.normed_two[mcot_own, :] = (unit_two * gain_two).astype(bf)
+    until_two = wires.total
     for device in group:
         wires.send(k.normed_two.at[mcot_own], k.normed_two.at[mcot_own], in_two + own_slot, device)
+    load_down.wait()
+    z_cast(k.down.at[up_slot], k.down.at[up_slot], in_down + z)
 
     core_exchange(k.up, in_up)
     wires.wait(k.up.at[at((1 - c) * half, half)], in_up + LEVELS)
@@ -618,43 +661,11 @@
         lax.fori_loop(0, mlp_rows // tile, step, 0)
 
     hidden_tiles(own_slot)
-    mlp_relay(k.down, in_down)
     for slot in group_slot:
+        if slot is group_slot[2]:
+            mlp_relay(k.down, in_down)
         wires.wait(k.normed_two.at[at(slot * rows, rows)], in_two + slot)
         hidden_tiles(slot)
-
-    core_exchange(k.down, in_down)
-    wires.wait(k.down.at[at((1 - c) * half, half)], in_down + LEVELS)
-    for slot in group_slot:
-        wires.wait(k.mixed_cot.at[at(slot * rows, rows)], in_mcot + slot)
-
-    def cot_tiles(slot):
-        here = at(slot * rows, rows)
-
-        def step(n, unused):
-            cols = at(n * tile, tile)
-            up_to = dot_inner(k.mixed_cot[here, :], k.down[cols, :])
-            k.hid_cot[here, cols] = (up_to * k.slope[here, cols]).astype(bf)
-            return unused
-
-        lax.fori_loop(0, mlp_rows // tile, step, 0)
-
-    def part_tiles(left, right, slot, dst):
-        here = at(slot * rows, rows)
-
-        def step(n, unused):
-            cols = at(n * tile, tile)
-            dst[:, cols] = dot_nn(left[here, :], right[:, cols]).astype(dst.dtype)
-            return unused
-
-        lax.fori_loop(0, width // tile, step, 0)
-
-    for i in (2, 0, 1):
-        cot_tiles(group_slot[i])
-        part_tiles(k.hid_cot, k.up, group_slot[i], k.part_out.at[0, i])
-        wires.send(k.part_out.at[0, i], k.part_in.at[0, own_slot], in_part[0] + own_slot, group[i])
-    cot_tiles(own_slot)
-    part_tiles(k.hid_cot, k.up, own_slot, k.part_own.at[0])
 
     def grad_tiles(left, right, start, dst):
         def step(n, unused):
@@ -664,12 +675,17 @@
 
         lax.fori_loop(0, half // tile, step, 0)
 
-    pairs = ((k.act, k.mixed_cot), (k.hid_cot, k.normed_two))
     passed = []
-    for which, (left, right) in enumerate(pairs):
+
+    def grad_halves(which, left, right):
         grad_tiles(left, right, (1 - c) * half, k.grad_pass.at[which])
         passed.append(wires.send(k.grad_pass.at[which], k.grad_core.at[which], in_core[which], (c_s, v)))
         grad_tiles(left, right, c * half, k.grad_keep.at[which])
+
+    for slot in group_slot:
+        wires.wait(k.mixed_cot.at[at(slot * rows, rows)], in_mcot + slot)
+    grad_halves(0, k.act, k.mixed_cot)
+    core_exchange(k.down, in_down)
 
     def grad_level(which, zt):
         there = at(zt * hidden, hidden)
@@ -689,8 +705,8 @@
 
     def send_far(which):
         via = LEVELS
+        wires.send(grad_piece(which, z_flip), k.grad_in.at[which, via], in_grad[which] + via, level(z_pair), when=outer)
         wires.send(grad_piece(which, z_two), k.grad_in.at[which, z], in_grad[which] + z, level(z_two), when=outer)
-        wires.send(grad_piece(which, z_flip), k.grad_in.at[which, via], in_grad[which] + via, level(z_pair), when=outer)
         wires.send(grad_piece(which, z_flip), k.grad_in.at[which, z], in_grad[which] + z, level(z_flip), when=inner)
 
     def send_joined(which):
@@ -716,7 +732,35 @@
             dst[...] = dst[...] + k.grad_in[which, z_flip].astype(f3)
 
     add_cores(0)
+    send_far(0)
     send_near(0)
+
+    wires.wait(k.down.at[at((1 - c) * half, half)], in_down + LEVELS)
+
+    def cot_tile(n, unused):
+        cols = at(n * tile, tile)
+        up_to = dot_inner(k.mixed_cot[...], k.down[cols, :])
+        k.hid_cot[:, cols] = (up_to * k.slope[:, cols]).astype(bf)
+        return unused
+
+    lax.fori_loop(0, mlp_rows // tile, cot_tile, 0)
+
+    def part_tiles(which, left, right):
+        def step(n, unused):
+            cols = at(n * tile, tile)
+            k.part_all[:, cols] = dot_nn(left[...], right[:, cols])
+            return unused
+
+        lax.fori_loop(0, width // tile, step, 0)
+        for i in (2, 0, 1):
+            k.part_out[which, i] = k.part_all[at(group_slot[i] * rows, rows), :].astype(bf)
+            wires.send(k.part_out.at[which, i], k.part_in.at[which, own_slot], in_part[which] + own_slot, group[i])
+        k.part_own[which] = k.part_all[mcot_own, :]
+
+    part_tiles(0, k.hid_cot, k.up)
+    grad_halves(1, k.hid_cot, k.normed_two)
+    part_tiles(1, k.act, k.down)
+    send_joined(0)
 
     def part_sum(which):
         total = k.part_own[which]
@@ -726,7 +770,9 @@
         return total
 
     unit_two, inverse_two = norm_stats(k.middle[...])
+    wires.settle(until_two)
     cot_two = part_sum(0)
+    until_acot = wires.total
     k.gain_own[1:2, :] = jnp.sum(cot_two * unit_two, axis=0, keepdims=True)
     middle_cot = out_cot[...].astype(f3) + norm_back(cot_two, unit_two, inverse_two, gain_two)
     tokens_grad[...] = middle_cot
@@ -736,9 +782,10 @@
             k.branch[...], k.wo[pl.ds(n * tile, tile), :]
         ).astype(bf)
     for p in view_peers:
-        wires.send(k.acot_tok.at[:, at(p * own, own)], view_rows(k.acot, v), in_acot + v, (s, p))
+        wires.send(k.acot_tok.at[:, at(p * own, own)], view_rows(k.acot, v), in_acot + v, (s, p), bulk=to_view[2])
     k.acot[at(v * rows, rows), :] = k.acot_tok[:, own_cols]
-    send_far(0)
+    add_cores(1)
+    send_near(1)
 
     o_half, o_quarter, o_eighth = width // 2, width // 4, width // 8
     o_piece = o_eighth // LEVELS
@@ -755,10 +802,6 @@
     outer_rows((1 - c) * o_half, k.do_core, bf)
     wires.send(k.do_core, k.do_core_in, in_do, (c_s, v))
     outer_rows(c * o_half, k.do_keep, f3)
-    for i in (2, 0, 1):
-        part_tiles(k.act, k.down, group_slot[i], k.part_out.at[1, i])
-        wires.send(k.part_out.at[1, i], k.part_in.at[1, own_slot], in_part[1] + own_slot, group[i])
-    part_tiles(k.act, k.down, own_slot, k.part_own.at[1])
     wires.wait(k.do_core_in, in_do)
     k.do_keep[...] = k.do_keep[...] + k.do_core_in[...].astype(f3)
     k.do_y[...] = k.do_keep[at((1 - y) * o_quarter, o_quarter), :].astype(bf)
@@ -804,29 +847,34 @@
 
     lax.fori_loop(0, count, unsort, 0, unroll=8)
     for p in view_peers:
-        wires.send(k.pc.at[:, at(p * rows, rows)], k.pc_tok.at[:, :, own_cols], in_pc + v, (s, p))
+        wires.send(k.pc.at[:, at(p * rows, rows)], k.pc_tok.at[:, :, own_cols], in_pc + v, (s, p), bulk=to_view[3])
     for t in range(3):
         k.pc_tok[t, :, own_cols] = k.pc[t, at(v * rows, rows), :]
 
     part = width // seqs
-    for i, p in enumerate(seq_peers):
+
+    def own_dw(row_block, t):
+        return dot_outer(k.normed[:, at(row_block * part, part)], k.pc[t])
+
+    for i, xt in enumerate((1 - x, x)):
         for t in range(3):
-            k.dw_out[i, t] = dot_outer(k.normed[:, at(p * part, part)], k.pc[t]).astype(bf)
-        wires.send(k.dw_out.at[i], k.dw_in.at[s], in_dw + s, (p, v))
-    own_part = at(s * part, part)
-    own_dw = [dot_outer(k.normed[:, own_part], k.pc[t]) for t in range(3)]
-    send_joined(0)
+            k.dw_out[i, t] = own_dw(xt * 2 + 1 - c, t).astype(bf)
+        wires.send(k.dw_out.at[i], k.dw_in.at[i], in_dw + i, (c_s, v))
+    wires.wait(k.dw_in.at[0], in_dw)
+    for t in range(3):
+        k.dw_x[t] = (own_dw(x_s, t) + k.dw_in[0, t].astype(f3)).astype(bf)
+    wires.send(k.dw_x, k.dw_in.at[2], in_dw + 2, (x_s, v))
     wires.wait(k.do_y_in, in_do + 1)
     o_mine = at(y * o_quarter, o_quarter)
     k.do_keep[o_mine, :] = k.do_keep[o_mine, :] + k.do_y_in[...].astype(f3)
     k.do_x[...] = k.do_keep[at(y * o_quarter + (1 - x) * o_eighth, o_eighth), :].astype(bf)
     wires.send(k.do_x, k.do_x_in, in_do + 2, (x_s, v))
-    for p in seq_peers:
-        wires.wait(k.dw_in.at[p], in_dw + p)
+    mine_dw = [own_dw(s, t) for t in range(3)]
+    wires.wait(k.dw_in.at[1], in_dw + 1)
+    wires.settle(until_acot)
+    wires.wait(k.dw_in.at[2], in_dw + 2)
     for t in range(3):
-        total = own_dw[t]
-        for p in seq_peers:
-            total = total + k.dw_in[p, t].astype(f3)
+        total = mine_dw[t] + k.dw_in[1, t].astype(f3) + k.dw_in[2, t].astype(f3)
         k.dw_own[t] = total.astype(bf)
 
     def w_at(q, j, first, last):
@@ -845,27 +893,13 @@
     wires.send(k.dw_own, w_plane(v), in_plane + v, (s, y_v))
     z_cast(k.dw_own, w_plane(v), in_plane + v)
     wires.send(k.dw_own.at[pl.ds(1, 2)], w_cross(s, v), in_cross + v, (x_s, v))
-    wires.send(k.dw_own, w_plane(v), in_mate[0] + v, (c_s, v))
-    keep_w = load(k.dw_own, w_plane(v))
+    wires.send(k.dw_own, w_plane(v), in_mate[0], (c_s, v), bulk=to_mate_w[0])
+    kept.append(load(k.dw_own, w_plane(v)))
 
     wires.wait(w_query(v), in_query + v)
     wires.send(w_query(v), w_query(v), in_query + v, (s, y_v))
     z_cast(w_query(v), w_query(v), in_query + v)
-    wires.send(w_query(v), w_query(v), in_mate[1] + v, (c_s, v))
-
-    wires.wait(k.do_x_in, in_do + 2)
-    total = k.do_keep[at(y * o_quarter + x * o_eighth, o_eighth), :] + k.do_x_in[...].astype(f3)
-    k.do_z[...] = total.astype(bf)
-
-    def o_level(zt):
-        return at(zt * o_piece, o_piece)
-
-    for zt in others_z:
-        wires.send(k.do_z.at[o_level(zt)], k.do_z_in.at[z], in_do_z + z, level(zt))
-
-    add_cores(1)
-    send_near(1)
-    send_far(1)
+    wires.send(w_query(v), w_query(v), in_mate[1], (c_s, v), bulk=to_mate_w[1])
 
     load_w.wait()
     for p in view_peers:
@@ -887,13 +921,14 @@
     tokens_grad[...] = tokens_grad[...] + norm_back(cot_one, unit_one, inverse_one, gain_one)
     for p in seq_peers:
         wires.send(k.gain_own, k.gain_in.at[s], in_gain + s, (p, v))
+    kept.append(load(tokens_grad, tokens_hbm))
 
     def o_at(q, j):
         at_c, at_x, at_y, at_z = q % 2, q // 2, j % 2, j // 2
         return o_grad.at[at(at_c * o_half + at_y * o_quarter + at_x * o_eighth + at_z * o_piece, o_piece)]
 
-    def to_mate(which, ref, j):
-        wires.send(ref, ref, in_mate[which] + j, (c_s, v))
+    def to_mate(which, ref):
+        wires.send(ref, ref, in_mate[which], (c_s, v), bulk=to_mate_w[which])
 
     def pass_plane(zt, row_y):
         j = zt * 2 + row_y
@@ -903,7 +938,7 @@
                 z_relay(w_plane(j), in_plane + j)
             wires.send(w_plane(j), w_plane(j), in_plane + j, (s, y_v))
         wires.send(w_cross(s, j), w_cross(s, j), in_cross + j, (x_s, v))
-        to_mate(0, w_plane(j), j)
+        to_mate(0, w_plane(j))
 
     def pass_query(zt, row_y):
         j = zt * 2 + row_y
@@ -912,27 +947,36 @@
             if zt is z_two:
                 z_relay(w_query(j), in_query + j)
             wires.send(w_query(j), w_query(j), in_query + j, (s, y_v))
-        to_mate(1, w_query(j), j)
+        to_mate(1, w_query(j))
+
+    wires.wait(k.do_x_in, in_do + 2)
+    total = k.do_keep[at(y * o_quarter + x * o_eighth, o_eighth), :] + k.do_x_in[...].astype(f3)
+    k.do_z[...] = total.astype(bf)
+
+    def o_level(zt):
+        return at(zt * o_piece, o_piece)
+
+    for zt in others_z:
+        wires.send(k.do_z.at[o_level(zt)], k.do_z_in.at[z], in_do_z + z, level(zt))
 
     across = 1 - y
     for zt in others_z:
         pass_plane(zt, y)
-    pass_plane(z, across)
+    for zt in others_z:
+        pass_query(zt, y)
     total = k.do_keep[at(y * o_quarter + x * o_eighth + z * o_piece, o_piece), :]
     total = total + k.do_x_in[o_level(z), :].astype(f3)
     for zt in others_z:
         wires.wait(k.do_z_in.at[zt], in_do_z + zt)
         total = total + k.do_z_in[zt].astype(f3)
     k.do_own[...] = total.astype(bf)
-    wires.send(k.do_own, o_at(s, v), in_out + s * views + v, (s, y_v))
-    z_cast(k.do_own, o_at(s, v), in_out + s * views + v)
-    wires.send(k.do_own, o_at(s, v), in_out + s * views + v, (x_s, v))
-    wires.send(k.do_own, o_at(s, v), in_out + s * views + v, (c_s, v))
-    keep_o = load(k.do_own, o_at(s, v))
-    for zt in others_z:
-        pass_query(zt, y)
-    send_joined(1)
-    for zt in others_z:
+    wires.send(k.do_own, o_at(s, v), in_out[0] + v, (s, y_v))
+    z_cast(k.do_own, o_at(s, v), in_out[0] + v)
+    wires.send(k.do_own, o_at(s, v), in_out[1] + v, (x_s, v))
+    wires.send(k.do_own, o_at(s, v), in_out_mate, (c_s, v), bulk=to_mate_o)
+    kept.append(load(k.do_own, o_at(s, v)))
+    send_far(1)
+    for zt in [z] + others_z:
         pass_plane(zt, across)
     for zt in [z] + others_z:
         pass_query(zt, across)
@@ -943,30 +987,41 @@
         total = total + k.gain_in[p]
     k.gain_sum[...] = total
     for p in view_peers:
-        wires.send(k.gain_sum, k.gain_all.at[v], in_gains + v, (s, p))
-
-    def pass_out(q, j, devices, relay):
-        slot = in_out + q * views + j
-        wires.wait(o_at(q, j), slot)
-        if relay:
-            z_relay(o_at(q, j), slot)
-        for device in devices:
-            wires.send(o_at(q, j), o_at(q, j), slot, device)
+        wires.send(k.gain_sum, k.gain_all.at[v], in_gains + v, (s, p), bulk=to_view[4])
+
+    def out_mate(q, j):
+        wires.send(o_at(q, j), o_at(q, j), in_out_mate, (c_s, v), bulk=to_mate_o)
+
+    def pass_out(zt, row_y):
+        j = zt * 2 + row_y
+        slot = in_out[0] + j
+        wires.wait(o_at(s, j), slot)
+        if row_y is y:
+            if zt is z_two:
+                z_relay(o_at(s, j), slot)
+            wires.send(o_at(s, j), o_at(s, j), slot, (s, y_v))
+        wires.send(o_at(s, j), o_at(s, j), in_out[1] + j, (x_s, v))
+        out_mate(s, j)
 
     for zt in others_z:
-        pass_out(s, zt * 2 + y, [(s, y_v), (x_s, v), (c_s, v)], zt is z_two)
+        pass_out(zt, y)
+    send_joined(1)
     for zt in [z] + others_z:
-        pass_out(s, zt * 2 + across, [(x_s, v), (c_s, v)], False)
+        pass_out(zt, across)
 
     layer_out[...] = (k.middle[...] + live * part_sum(1)).astype(bf)
+    kept.append(load(layer_out, layer_hbm))
     collect(0, down_grad)
+    kept.append(load(down_grad, down_hbm_out))
     by_arrival = [v] + [zt * 2 + y for zt in others_z] + [zt * 2 + across for zt in [z] + others_z]
     for j in by_arrival:
         wires.wait(w_cross(x_s, j), in_cross + j)
-        to_mate(2, w_cross(x_s, j), j)
+        to_mate(2, w_cross(x_s, j))
     for j in by_arrival:
-        pass_out(x_s, j, [(c_s, v)], False)
+        wires.wait(o_at(x_s, j), in_out[1] + j)
+        out_mate(x_s, j)
     collect(1, up_grad)
+    kept.append(load(up_grad, up_hbm_out))
 
     total = k.gain_sum[...]
     for p in view_peers:
@@ -974,30 +1029,72 @@
         total = total + k.gain_all[p]
     gains[...] = total
 
-    for j in range(views):
-        wires.wait(w_at(c_s, j, 0, 3), in_mate[0] + j)
-        wires.wait(w_at(xc_s, j, 0, 1), in_mate[1] + j)
-        wires.wait(w_cross(xc_s, j), in_mate[2] + j)
-        for q in (c_s, xc_s):
-            wires.wait(o_at(q, j), in_out + q * views + j)
-    keep_w.wait()
-    keep_o.wait()
-    wires.drain()
+    def w_rows(q, first, last):
+        return w_grad.at[pl.ds(first, last - first), at(q * part, part)]
+
+    def o_core(core):
+        return o_grad.at[at(core * o_half, o_half)]
+
+    wires.settle(wires.total)
+    for whole, lane in (
+        (k.ids_all.at[pl.ds(0, views - 1)], to_view[0]),
+        (k.att.at[pl.ds(0, length - rows)], to_view[1]),
+        (k.acot.at[pl.ds(0, length - rows)], to_view[2]),
+        (k.pc.at[:, pl.ds(0, length - rows)], to_view[3]),
+        (k.gain_all.at[pl.ds(0, views - 1)], to_view[4]),
+        (w_rows(s, 0, 3), to_mate_w[0]),
+        (w_rows(x_s, 0, 1), to_mate_w[1]),
+        (w_rows(x_s, 1, 3), to_mate_w[2]),
+        (o_core(c), to_mate_o),
+    ):
+        wires.settle_bulk(whole, lane)
+    wires.wait(w_rows(c_s, 0, 3), in_mate[0])
+    wires.wait(w_rows(xc_s, 0, 1), in_mate[1])
+    wires.wait(w_rows(xc_s, 1, 3), in_mate[2])
+    wires.wait(o_core(1 - c), in_out_mate)
+    for copy in kept:
+        copy.wait()
+
+
+FINISH_STEPS = 8
 
 
 def finish_kernel(*refs):
     (layer_in, tokens_in, gains, w_in, o_in, up_in, down_in) = refs[:7]
-    (layer_out, tokens_grad, gain_one, w_out, o_out, gain_two, up_out, down_out) = refs[7:]
-    width = w_in.shape[2]
-    for t in range(3):
-        w_out[:, t * width : (t + 1) * width] = w_in[t].astype(jnp.float32)
-    o_out[...] = o_in[...].astype(jnp.float32)
-    layer_out[...] = layer_in[...]
-    tokens_grad[...] = tokens_in[...]
-    up_out[...] = up_in[...]
-    down_out[...] = down_in[...]
+    (layer_out, tokens_grad, gain_one, w_out, o_out, gain_two, up_out, down_out) = refs[7:15]
+    (layer, tokens, up, down, w_narrow, o_narrow, w_wide, o_wide, in_sem, out_sem) = refs[15:]
+    width = o_in.shape[0]
+    tall = width // FINISH_STEPS
+    asis = ((layer_in, layer, layer_out), (tokens_in, tokens, tokens_grad), (up_in, up, up_out), (down_in, down, down_out))
+
+    def rows(i):
+        return pl.ds(i * tall, tall)
+
+    def start(src, dst, sem):
+        copy = pltpu.make_async_copy(src, dst, sem)
+        copy.start()
+        return copy
+
+    reads, writes = [], []
+    for i in range(FINISH_STEPS):
+        reads.append(start(w_in.at[:, rows(i)], w_narrow.at[:, rows(i)], in_sem.at[2 * i]))
+        reads.append(start(o_in.at[rows(i)], o_narrow.at[rows(i)], in_sem.at[2 * i + 1]))
+    late = [start(src, mid, in_sem.at[2 * FINISH_STEPS + i]) for i, (src, mid, dst) in enumerate(asis)]
     gain_one[...] = gains[0:1, :].reshape(width)
     gain_two[...] = gains[1:2, :].reshape(width)
+    for i in range(FINISH_STEPS):
+        reads[2 * i].wait()
+        for t in range(3):
+            w_wide[rows(i), t * width : (t + 1) * width] = w_narrow[t, rows(i), :].astype(jnp.float32)
+        writes.append(start(w_wide.at[rows(i)], w_out.at[rows(i)], out_sem.at[2 * i]))
+        reads[2 * i + 1].wait()
+        o_wide[rows(i), :] = o_narrow[rows(i), :].astype(jnp.float32)
+        writes.append(start(o_wide.at[rows(i)], o_out.at[rows(i)], out_sem.at[2 * i + 1]))
+    for i, (src, mid, dst) in enumerate(asis):
+        late[i].wait()
+        writes.append(start(mid, dst, out_sem.at[2 * FINISH_STEPS + i]))
+    for copy in writes:
+        copy.wait()
 
 
 def fused(
@@ -1032,8 +1129,8 @@
             shape((hidden, width), f3),
             shape((hidden, width), f3),
         ),
-        in_specs=[vmem] * 6 + [anywhere] * 4,
-        out_specs=(vmem, vmem, vmem, anywhere, anywhere, vmem, vmem),
+        in_specs=[anywhere, vmem, vmem, anywhere, vmem, vmem] + [anywhere] * 4,
+        out_specs=(anywhere, anywhere, vmem, anywhere, anywhere, anywhere, anywhere),
         scratch_shapes=list(spec.values()),
         compiler_params=pltpu.CompilerParams(
             collective_id=0, has_side_effects=True, vmem_limit_bytes=67043328
@@ -1051,19 +1148,8 @@
         up_weight,
         down_weight,
     )
-    steps = 8
-
-    def slab(*lead):
-        full = lead + (width,)
-        block = full[:-2] + (full[-2] // steps, width)
-        return pl.BlockSpec(block, lambda i: (0,) * (len(block) - 2) + (i, 0))
-
-    whole = pl.BlockSpec((8, width), lambda i: (0, 0))
-    line = pl.BlockSpec((width,), lambda i: (0,))
-    thick = pl.BlockSpec((width // steps, 3 * width), lambda i: (i, 0))
     layer_out, tokens_grad, gain_one, w_grad, o_grad, gain_two, up_grad, down_grad = pl.pallas_call(
         finish_kernel,
-        grid=(steps,),
         out_shape=(
             shape((rows, width), bf),
             shape((rows, width), f3),
@@ -1074,8 +1160,20 @@
             shape((hidden, width), f3),
             shape((hidden, width), f3),
         ),
-        in_specs=[slab(rows), slab(rows), whole, slab(3, width), slab(width), slab(hidden), slab(hidden)],
-        out_specs=(slab(rows), slab(rows), line, thick, slab(width), line, slab(hidden), slab(hidden)),
+        in_specs=[anywhere] * 2 + [vmem] + [anywhere] * 4,
+        out_specs=(anywhere, anywhere, vmem, anywhere, anywhere, vmem, anywhere, anywhere),
+        scratch_shapes=[
+            pltpu.VMEM((rows, width), bf),
+            pltpu.VMEM((rows, width), f3),
+            pltpu.VMEM((hidden, width), f3),
+            pltpu.VMEM((hidden, width), f3),
+            pltpu.VMEM((3, width, width), bf),
+            pltpu.VMEM((width, width), bf),
+            pltpu.VMEM((width, 3 * width), f3),
+            pltpu.VMEM((width, width), f3),
+            pltpu.SemaphoreType.DMA((2 * FINISH_STEPS + 4,)),
+            pltpu.SemaphoreType.DMA((2 * FINISH_STEPS + 4,)),
+        ],
         name="finish",
     )(*parts)
     return (

time: 204 us -> 190 us (0.931)
  Pallas kernels: 203 us -> 188 us
    pallas_call x1, Pallas kernels: 192 us -> 177 us  [fused(): pl.pallas_call(functools.partial(layer_kernel, tuple(spec), seqs, views),...]
where the time goes in v3:
time: 190 us; the launch traced here: 189 us
  Pallas kernels  188 us (99%)
    pallas_call x1, Pallas kernels, fused(): pl.pallas_call(functools.partial(layer_kernel, tuple(spec), seqs, views),...  177 us
    pallas_call x1, Pallas kernels, fused(): pl.pallas_call(finish_kernel, out_shape=(shape((rows, width), bf), shape(...  10.8 us

profile of v3, /device:TPU:0, one launch (start us, length us, event | category | flops | bytes accessed | tf_op | source)
XLA Modules:
  0.0 188.7 jit_solution(12956108319040224676)
XLA Ops:
  0.6 177.1 %layer.1 = (bf16[128,1024]{1,0:T(8,128)(2,1)}, f32[128,1024]{1,0:T(8,128)}, f32[8,1024]{1,0:T(8,128)}, bf16[3,1024,1024]{2,1,0:T(8,128)(2,1)}, bf16[1024,1024]{1...) custom-call(bf16[128,1024]{1,0:T(8,128)(2,1)} %bitcast.4, s32[1,128]{1,0:T(1,128)} %refs_1_.1, ...), custom_call_target="tpu_custom_call" | custom-call | tf_op jit(solution)/shard_map/layer/pallas_call | solution.py:1121
  177.7 10.8 %finish.1 = (bf16[128,1024]{1,0:T(8,128)(2,1)}, f32[128,1024]{1,0:T(8,128)}, f32[1024]{0:T(1024)}, f32[1024,3072]{1,0:T(8,128)}, f32[1024,1024]{1,0:T(8,128)}, /...) custom-call(bf16[128,1024]{1,0:T(8,128)(2,1)} %get-tuple-element.23.refs_0_, ...), custom_call_target="tpu_custom_call" | custom-call | tf_op jit(solution)/shard_map/finish/pallas_call | solution.py:1151

commit v4 on v3

--- a/solution.py
+++ b/solution.py
@@ -320,7 +320,7 @@
         self.copy(dst, dst, 0, slot, self.peer).wait_recv()
 
 
-SENDS, RECVS, LOCALS = 80, 124, 16
+SENDS, RECVS, LOCALS = 88, 136, 20
 LEVELS = 4
 
 
@@ -357,29 +357,29 @@
         middle=vm((rows, width), f3),
         normed_two=vm((4 * rows, width), bf),
         mixed_cot=vm((4 * rows, width), bf),
-        slope=vm((4 * rows, mlp_rows), f3),
-        part_all=vm((4 * rows, width), f3),
+        wide=vm((4 * rows, mlp_rows), f3),
         act=vm((4 * rows, mlp_rows), bf),
         hid_cot=vm((4 * rows, mlp_rows), bf),
-        part_own=vm((2, rows, width), f3),
+        part_own=vm((2, 2, rows, width), f3),
         part_out=vm((2, 3, rows, width), bf),
-        part_in=vm((2, 4, rows, width), bf),
+        part_in=vm((2, 3, rows, width), bf),
         grad_keep=vm((2, mlp_rows // 2, width), bf),
         grad_pass=vm((2, mlp_rows // 2, width), bf),
         grad_core=vm((2, mlp_rows // 2, width), bf),
-        grad_in=vm((2, LEVELS + 1, hidden, width), bf),
+        grad_y=vm((2, 2, hidden, width), bf),
+        grad_z=vm((2, hidden, width), bf),
         branch=vm((rows, width), bf),
         acot_tok=vm((rows, width), bf),
         acot=vm((length, own), bf),
         acot_s=vm((length, own), bf),
         pc_s=vm((length, 3 * own), bf),
         pc=vm((3, length, own), bf),
+        pc_flat=vm((length, 3 * own), bf),
         pc_tok=vm((3, rows, width), bf),
         dw_out=vm((2, 3, width // seqs, own), bf),
         dw_x=vm((3, width // seqs, own), bf),
         dw_in=vm((3, 3, width // seqs, own), bf),
         dw_own=vm((3, width // seqs, own), bf),
-        do_keep=vm((half, width), f3),
         do_core=vm((half, width), bf),
         do_core_in=vm((half, width), bf),
         do_y=vm((quarter, width), bf),
@@ -401,8 +401,9 @@
 
 def layer_kernel(names, seqs, views, *refs):
     (tok_hbm, ids, alive, cot_hbm, gain_one_ref, gain_two_ref, w_hbm, wo_hbm, up_hbm, down_hbm) = refs[:10]
-    (layer_hbm, tokens_hbm, gains, w_grad, o_grad, up_hbm_out, down_hbm_out) = refs[10:17]
-    k = types.SimpleNamespace(**dict(zip(names, refs[17:])))
+    (layer_hbm, tokens_hbm, gains, w_grad, o_grad, up_part, up_away, down_hbm_out) = refs[10:18]
+    k = types.SimpleNamespace(**dict(zip(names, refs[18:])))
+    k.slope = k.part_all = k.do_keep = k.wide
     tok, out_cot = k.tok, k.out_cot
     layer_out, tokens_grad, up_grad, down_grad = k.layer_out, k.tokens_grad, k.up_grad, k.down_grad
     rows, width = tok.shape
@@ -423,11 +424,11 @@
     y_v = z * 2 + (1 - y)
     z_pair, z_two, z_flip = z + 1 - 2 * (z % 2), lax.rem(z + 2, LEVELS), LEVELS - 1 - z
     inner = (z == 1) | (z == 2)
-    outer = (z == 0) | (z == 3)
     others_z = [z_pair, z_two, z_flip]
-    group = [(x_s, v), (s, y_v), (x_s, y_v)]
-    group_slot = [(1 - x) * 2 + y, x * 2 + (1 - y), (1 - x) * 2 + (1 - y)]
-    own_slot = x * 2 + y
+    low, high = z % 2, z // 2
+    pair_v = z_pair * 2 + y
+    own_slot, x_slot = x * 2 + low, (1 - x) * 2 + low
+    pair_slot, far_slot = x * 2 + (1 - low), (1 - x) * 2 + (1 - low)
     view_peers = [lax.rem(v + d, views) for d in range(1, views)]
     seq_peers = [x_s, xc_s, c_s]
 
@@ -435,16 +436,16 @@
         return (s, zt * 2 + y)
 
     wires = Wires(k.send_sem, k.recv_sem, (c_s, v))
-    in_normed = wires.inbox(views)
+    in_normed = wires.inbox(2 * views)
     in_ids = wires.inbox(views)
     in_up = wires.inbox(LEVELS + 1)
     in_down = wires.inbox(LEVELS + 1)
     in_mcot = wires.inbox(4)
     in_att = wires.inbox(views)
     in_two = wires.inbox(4)
-    in_part = [wires.inbox(4), wires.inbox(4)]
+    in_part = [wires.inbox(5), wires.inbox(5)]
     in_core = [wires.inbox(1), wires.inbox(1)]
-    in_grad = [wires.inbox(LEVELS + 1), wires.inbox(LEVELS + 1)]
+    in_grad = [wires.inbox(3), wires.inbox(3)]
     in_acot, in_pc = in_ids, in_att
     in_dw = wires.inbox(3)
     in_do = wires.inbox(3)
@@ -470,7 +471,7 @@
         wires.send(ref, ref, slot, level(z_pair), when=inner)
 
     barrier = pltpu.get_barrier_semaphore()
-    greeted = [(s, p) for p in view_peers] + [(p, v) for p in seq_peers] + [(x_s, y_v)]
+    greeted = [(s, p) for p in view_peers] + [(p, v) for p in seq_peers]
     for device in greeted:
         pl.semaphore_signal(barrier, inc=1, device_id=device, device_id_type=MESH)
 
@@ -482,7 +483,7 @@
         loads.append(copy)
         return copy
 
-    up_slot = at((c * LEVELS + z) * hidden, hidden)
+    up_slot = at((c * 4 + y * 2 + high) * hidden, hidden)
     load_tok = load(tok_hbm, tok)
     load_cot = load(cot_hbm, out_cot)
     load_up = load(up_hbm, k.up.at[up_slot])
@@ -514,17 +515,35 @@
 
     for p in view_peers:
         wires.send(k.ids_all.at[v], k.ids_all.at[v], in_ids + v, (s, p), bulk=to_view[0])
-    mine = view_rows(k.normed, v)
-    wires.send(mine, mine, in_normed + v, (s, y_v))
-    z_cast(mine, mine, in_normed + v)
+
+    def normed_half(j, i):
+        return k.normed.at[at(j * rows + i * (rows // 2), rows // 2)], in_normed + 2 * j + i
+
+    for i in range(2):
+        mine, slot = normed_half(v, i)
+        wires.send(mine, mine, slot, (s, y_v))
+    for zt in (z_pair, z_two):
+        for i in range(2):
+            mine, slot = normed_half(v, i)
+            wires.send(mine, mine, slot, level(zt))
+    for i in range(2):
+        mine, slot = normed_half(v, i)
+        wires.send(mine, mine, slot, level(z_flip), when=inner)
     load_cot.wait()
     mcot_own = at(own_slot * rows, rows)
     k.mixed_cot[mcot_own, :] = (live * out_cot[...].astype(f3)).astype(bf)
 
-    def send_mcot(device):
-        wires.send(k.mixed_cot.at[mcot_own], k.mixed_cot.at[mcot_own], in_mcot + own_slot, device)
-
-    send_mcot(group[0])
+    def slot_rows(ref, slot):
+        return ref.at[at(slot * rows, rows)]
+
+    def square_send(ref, base, slot, device):
+        wires.send(slot_rows(ref, slot), slot_rows(ref, slot), base + slot, device)
+
+    def square_relay(ref, base):
+        wires.wait(slot_rows(ref, pair_slot), base + pair_slot)
+        square_send(ref, base, pair_slot, (x_s, v))
+
+    square_send(k.mixed_cot, in_mcot, own_slot, (x_s, v))
 
     for p in view_peers:
         wires.wait(k.ids_all.at[p], in_ids + p)
@@ -548,48 +567,47 @@
     for copy in load_own:
         copy.wait()
 
+    def mlp_slot(ref, yt, ht):
+        return ref.at[at((c * 4 + yt * 2 + ht) * hidden, hidden)]
+
+    def send_mlp(ref, base, device):
+        mine = mlp_slot(ref, y, high)
+        wires.send(mine, mine, base + y * 2 + high, device)
+
+    def mlp_relay(ref, base):
+        there = mlp_slot(ref, y, 1 - high)
+        wires.wait(there, base + y * 2 + 1 - high)
+        wires.send(there, there, base + y * 2 + 1 - high, (s, y_v))
+
+    def core_exchange(ref, base):
+        for ht in (high, 1 - high):
+            wires.wait(mlp_slot(ref, 1 - y, ht), base + (1 - y) * 2 + ht)
+        mine = ref.at[at(c * half, half)]
+        wires.send(mine, mine, base + LEVELS, (c_s, v))
+
     def project(j):
         k.qkv[at(j * rows, rows), :] = dot_nn(k.normed[at(j * rows, rows), :], k.w_own[...]).astype(bf)
 
     project(v)
     for zt in others_z:
         j = zt * 2 + y
-        there = view_rows(k.normed, j)
-        wires.wait(there, in_normed + j)
-        if zt is z_two:
-            z_relay(there, in_normed + j)
-        wires.send(there, there, in_normed + j, (s, y_v))
+        for i in range(2):
+            there, slot = normed_half(j, i)
+            wires.wait(there, slot)
+            if zt is z_two:
+                z_relay(there, slot)
+            wires.send(there, there, slot, (s, y_v))
         if zt is z_two:
             load_up.wait()
-            z_cast(k.up.at[up_slot], k.up.at[up_slot], in_up + z)
+            send_mlp(k.up, in_up, level(z_two))
+            square_send(k.mixed_cot, in_mcot, own_slot, (s, pair_v))
         project(j)
+    send_mlp(k.up, in_up, (s, y_v))
     for zt in [z] + others_z:
         j = zt * 2 + 1 - y
-        wires.wait(view_rows(k.normed, j), in_normed + j)
+        for i in range(2):
+            wires.wait(*normed_half(j, i))
         project(j)
-    def mlp_slot(ref, zt):
-        return ref.at[at((c * LEVELS + zt) * hidden, hidden)]
-
-    def mlp_relay(ref, base):
-        @pl.when(inner)
-        def _():
-            wires.wait(mlp_slot(ref, z_two), base + z_two)
-
-        z_relay(mlp_slot(ref, z_two), base + z_two)
-
-    def core_exchange(ref, base):
-        @pl.when(outer)
-        def _():
-            wires.wait(mlp_slot(ref, z_two), base + z_two)
-
-        for zt in (z_pair, z_flip):
-            wires.wait(mlp_slot(ref, zt), base + zt)
-        mine = ref.at[at(c * half, half)]
-        wires.send(mine, mine, base + LEVELS, (c_s, v))
-
-    mlp_relay(k.up, in_up)
-    send_mcot(group[1])
-    send_mcot(group[2])
     to_scalar.wait()
 
     def reorder(dst, src, row):
@@ -626,6 +644,11 @@
     own_cols = at(v * own, own)
     for p in view_peers:
         wires.send(view_rows(k.att, p), k.att_tok.at[:, own_cols], in_att + v, (s, p), bulk=to_view[1])
+    square_relay(k.mixed_cot, in_mcot)
+    mlp_relay(k.up, in_up)
+    load_down.wait()
+    send_mlp(k.down, in_down, level(z_two))
+    send_mlp(k.down, in_down, (s, y_v))
     k.att_tok[:, own_cols] = k.att[at(v * rows, rows), :]
 
 
@@ -639,10 +662,8 @@
     unit_two, _ = norm_stats(k.middle[...])
     k.normed_two[mcot_own, :] = (unit_two * gain_two).astype(bf)
     until_two = wires.total
-    for device in group:
-        wires.send(k.normed_two.at[mcot_own], k.normed_two.at[mcot_own], in_two + own_slot, device)
-    load_down.wait()
-    z_cast(k.down.at[up_slot], k.down.at[up_slot], in_down + z)
+    for device in ((s, pair_v), (x_s, v)):
+        square_send(k.normed_two, in_two, own_slot, device)
 
     core_exchange(k.up, in_up)
     wires.wait(k.up.at[at((1 - c) * half, half)], in_up + LEVELS)
@@ -661,10 +682,11 @@
         lax.fori_loop(0, mlp_rows // tile, step, 0)
 
     hidden_tiles(own_slot)
-    for slot in group_slot:
-        if slot is group_slot[2]:
-            mlp_relay(k.down, in_down)
-        wires.wait(k.normed_two.at[at(slot * rows, rows)], in_two + slot)
+    mlp_relay(k.down, in_down)
+    square_relay(k.normed_two, in_two)
+    hidden_tiles(pair_slot)
+    for slot in (x_slot, far_slot):
+        wires.wait(slot_rows(k.normed_two, slot), in_two + slot)
         hidden_tiles(slot)
 
     def grad_tiles(left, right, start, dst):
@@ -682,58 +704,38 @@
         passed.append(wires.send(k.grad_pass.at[which], k.grad_core.at[which], in_core[which], (c_s, v)))
         grad_tiles(left, right, c * half, k.grad_keep.at[which])
 
-    for slot in group_slot:
-        wires.wait(k.mixed_cot.at[at(slot * rows, rows)], in_mcot + slot)
+    for slot in (x_slot, far_slot):
+        wires.wait(slot_rows(k.mixed_cot, slot), in_mcot + slot)
+    core_exchange(k.down, in_down)
     grad_halves(0, k.act, k.mixed_cot)
-    core_exchange(k.down, in_down)
-
-    def grad_level(which, zt):
-        there = at(zt * hidden, hidden)
+
+    def grad_sum(which, start, size):
+        there = at(start, size)
         return k.grad_keep[which, there, :].astype(f3) + k.grad_core[which, there, :].astype(f3)
 
-    def grad_piece(which, zt):
-        return k.grad_pass.at[which, at(zt * hidden, hidden)]
-
-    def add_cores(which):
+    def grads_to_y(which):
         wires.wait(k.grad_core.at[which], in_core[which])
         wires.sent(passed[which])
-        for zt in others_z:
-            k.grad_pass[which, at(zt * hidden, hidden), :] = grad_level(which, zt).astype(bf)
-
-    def send_near(which):
-        wires.send(grad_piece(which, z_pair), k.grad_in.at[which, z], in_grad[which] + z, level(z_pair))
-
-    def send_far(which):
-        via = LEVELS
-        wires.send(grad_piece(which, z_flip), k.grad_in.at[which, via], in_grad[which] + via, level(z_pair), when=outer)
-        wires.send(grad_piece(which, z_two), k.grad_in.at[which, z], in_grad[which] + z, level(z_two), when=outer)
-        wires.send(grad_piece(which, z_flip), k.grad_in.at[which, z], in_grad[which] + z, level(z_flip), when=inner)
-
-    def send_joined(which):
-        @pl.when(inner)
-        def _():
-            wires.wait(k.grad_in.at[which, LEVELS], in_grad[which] + LEVELS)
-            there = at(z_two * hidden, hidden)
-            joined = k.grad_pass[which, there, :].astype(f3) + k.grad_in[which, LEVELS].astype(f3)
-            k.grad_pass[which, there, :] = joined.astype(bf)
-
-        wires.send(grad_piece(which, z_two), k.grad_in.at[which, z], in_grad[which] + z, level(z_two), when=inner)
+        for i, ht in enumerate((1 - high, high)):
+            start = ((1 - y) * 2 + ht) * hidden
+            there = at(start, hidden)
+            k.grad_pass[which, there, :] = grad_sum(which, start, hidden).astype(bf)
+            wires.send(k.grad_pass.at[which, there], k.grad_y.at[which, i], in_grad[which] + i, (s, y_v))
+
+    def grad_block(which, i, ht):
+        wires.wait(k.grad_y.at[which, i], in_grad[which] + i)
+        return grad_sum(which, (y * 2 + ht) * hidden, hidden) + k.grad_y[which, i].astype(f3)
+
+    def grads_to_z(which):
+        there = at((y * 2 + 1 - high) * hidden, hidden)
+        k.grad_pass[which, there, :] = grad_block(which, 0, 1 - high).astype(bf)
+        wires.send(k.grad_pass.at[which, there], k.grad_z.at[which], in_grad[which] + 2, level(z_two))
 
     def collect(which, dst):
-        total = grad_level(which, z)
-        for zt in (z_pair, z_two):
-            wires.wait(k.grad_in.at[which, zt], in_grad[which] + zt)
-            total = total + k.grad_in[which, zt].astype(f3)
-        dst[...] = total
-
-        @pl.when(inner)
-        def _():
-            wires.wait(k.grad_in.at[which, z_flip], in_grad[which] + z_flip)
-            dst[...] = dst[...] + k.grad_in[which, z_flip].astype(f3)
-
-    add_cores(0)
-    send_far(0)
-    send_near(0)
+        total = grad_block(which, 1, high)
+        wires.wait(k.grad_z.at[which], in_grad[which] + 2)
+        dst[...] = total + k.grad_z[which].astype(f3)
+
 
     wires.wait(k.down.at[at((1 - c) * half, half)], in_down + LEVELS)
 
@@ -745,28 +747,52 @@
 
     lax.fori_loop(0, mlp_rows // tile, cot_tile, 0)
 
+    strip = width // 2
+
+    def strip_cols(i):
+        return pl.ds(i * strip, strip)
+
     def part_tiles(which, left, right):
-        def step(n, unused):
-            cols = at(n * tile, tile)
-            k.part_all[:, cols] = dot_nn(left[...], right[:, cols])
-            return unused
-
-        lax.fori_loop(0, width // tile, step, 0)
-        for i in (2, 0, 1):
-            k.part_out[which, i] = k.part_all[at(group_slot[i] * rows, rows), :].astype(bf)
-            wires.send(k.part_out.at[which, i], k.part_in.at[which, own_slot], in_part[which] + own_slot, group[i])
-        k.part_own[which] = k.part_all[mcot_own, :]
-
+        for i in range(2):
+
+            def step(n, unused):
+                cols = at(i * strip + n * tile, tile)
+                k.part_all[:, cols] = dot_nn(left[...], right[:, cols])
+                return unused
+
+            lax.fori_loop(0, strip // tile, step, 0)
+            cols = strip_cols(i)
+            k.part_out[which, 0, :, cols] = k.part_all[at(far_slot * rows, rows), cols].astype(bf)
+            there = k.part_out.at[which, 0, :, cols], k.part_in.at[which, 0, :, cols]
+            wires.send(*there, in_part[which] + i, (x_s, v))
+        k.part_out[which, 1] = k.part_all[at(x_slot * rows, rows), :].astype(bf)
+        wires.send(k.part_out.at[which, 1], k.part_in.at[which, 1], in_part[which] + 2, (x_s, v))
+        for i, slot in enumerate((own_slot, pair_slot)):
+            k.part_own[which, i] = k.part_all[at(slot * rows, rows), :]
+
+    def part_join(which):
+        for i in range(2):
+            cols = strip_cols(i)
+            wires.wait(k.part_in.at[which, 0, :, cols], in_part[which] + i)
+            joined = k.part_own[which, 1, :, cols] + k.part_in[which, 0, :, cols].astype(f3)
+            k.part_out[which, 2, :, cols] = joined.astype(bf)
+            there = k.part_out.at[which, 2, :, cols], k.part_in.at[which, 2, :, cols]
+            wires.send(*there, in_part[which] + 3 + i, (s, pair_v))
+
+    grads_to_y(0)
     part_tiles(0, k.hid_cot, k.up)
     grad_halves(1, k.hid_cot, k.normed_two)
     part_tiles(1, k.act, k.down)
-    send_joined(0)
+    part_join(0)
+    grads_to_y(1)
 
     def part_sum(which):
-        total = k.part_own[which]
-        for slot in group_slot:
-            wires.wait(k.part_in.at[which, slot], in_part[which] + slot)
-            total = total + k.part_in[which, slot].astype(f3)
+        total = k.part_own[which, 0]
+        wires.wait(k.part_in.at[which, 1], in_part[which] + 2)
+        for i in range(2):
+            wires.wait(k.part_in.at[which, 2, :, strip_cols(i)], in_part[which] + 3 + i)
+        for i in (1, 2):
+            total = total + k.part_in[which, i].astype(f3)
         return total
 
     unit_two, inverse_two = norm_stats(k.middle[...])
@@ -784,8 +810,6 @@
     for p in view_peers:
         wires.send(k.acot_tok.at[:, at(p * own, own)], view_rows(k.acot, v), in_acot + v, (s, p), bulk=to_view[2])
     k.acot[at(v * rows, rows), :] = k.acot_tok[:, own_cols]
-    add_cores(1)
-    send_near(1)
 
     o_half, o_quarter, o_eighth = width // 2, width // 4, width // 8
     o_piece = o_eighth // LEVELS
@@ -809,6 +833,7 @@
 
     for p in view_peers:
         wires.wait(view_rows(k.acot, p), in_acot + p)
+    part_join(1)
     reorder(k.acot_s, k.acot, 0)
 
     def attend_back(g, unused):
@@ -841,6 +866,7 @@
 
     def unsort(i, unused):
         found = pc_blocks[k.order_sm[8, i]]
+        k.pc_flat[at(i * block, block), :] = found
         for t in range(3):
             k.pc[t, at(i * block, block), :] = found[:, t * own : (t + 1) * own]
         return unused
@@ -853,23 +879,20 @@
 
     part = width // seqs
 
-    def own_dw(row_block, t):
-        return dot_outer(k.normed[:, at(row_block * part, part)], k.pc[t])
+    def own_dw(row_block):
+        whole = dot_outer(k.normed[:, at(row_block * part, part)], k.pc_flat[...])
+        return [whole[:, t * own : (t + 1) * own] for t in range(3)]
 
     for i, xt in enumerate((1 - x, x)):
-        for t in range(3):
-            k.dw_out[i, t] = own_dw(xt * 2 + 1 - c, t).astype(bf)
+        for t, value in enumerate(own_dw(xt * 2 + 1 - c)):
+            k.dw_out[i, t] = value.astype(bf)
         wires.send(k.dw_out.at[i], k.dw_in.at[i], in_dw + i, (c_s, v))
+    cross_dw = own_dw(x_s)
     wires.wait(k.dw_in.at[0], in_dw)
     for t in range(3):
-        k.dw_x[t] = (own_dw(x_s, t) + k.dw_in[0, t].astype(f3)).astype(bf)
+        k.dw_x[t] = (cross_dw[t] + k.dw_in[0, t].astype(f3)).astype(bf)
     wires.send(k.dw_x, k.dw_in.at[2], in_dw + 2, (x_s, v))
-    wires.wait(k.do_y_in, in_do + 1)
-    o_mine = at(y * o_quarter, o_quarter)
-    k.do_keep[o_mine, :] = k.do_keep[o_mine, :] + k.do_y_in[...].astype(f3)
-    k.do_x[...] = k.do_keep[at(y * o_quarter + (1 - x) * o_eighth, o_eighth), :].astype(bf)
-    wires.send(k.do_x, k.do_x_in, in_do + 2, (x_s, v))
-    mine_dw = [own_dw(s, t) for t in range(3)]
+    mine_dw = own_dw(s)
     wires.wait(k.dw_in.at[1], in_dw + 1)
     wires.settle(until_acot)
     wires.wait(k.dw_in.at[2], in_dw + 2)
@@ -901,28 +924,11 @@
     z_cast(w_query(v), w_query(v), in_query + v)
     wires.send(w_query(v), w_query(v), in_mate[1], (c_s, v), bulk=to_mate_w[1])
 
-    load_w.wait()
-    for p in view_peers:
-        wires.wait(k.pc_tok.at[:, :, at(p * own, own)], in_pc + p)
-
-    def back_tile(n, unused):
-        cols = at(n * tile, tile)
-        total = dot_inner(k.pc_tok[0], k.w_full[cols, pl.ds(0, width)])
-        for t in range(1, 3):
-            total = total + dot_inner(k.pc_tok[t], k.w_full[cols, pl.ds(t * width, width)])
-        k.part_own[0, :, cols] = total
-        return unused
-
-    lax.fori_loop(0, width // tile, back_tile, 0)
-    unit_one, inverse_one = norm_stats(tok[...].astype(f3))
-    cot_one = k.part_own[0]
-    k.gain_own[0:1, :] = jnp.sum(cot_one * unit_one, axis=0, keepdims=True)
-    k.gain_own[2:8, :] = jnp.zeros((6, width), f3)
-    tokens_grad[...] = tokens_grad[...] + norm_back(cot_one, unit_one, inverse_one, gain_one)
-    for p in seq_peers:
-        wires.send(k.gain_own, k.gain_in.at[s], in_gain + s, (p, v))
-    kept.append(load(tokens_grad, tokens_hbm))
-
+    wires.wait(k.do_y_in, in_do + 1)
+    o_mine = at(y * o_quarter, o_quarter)
+    k.do_keep[o_mine, :] = k.do_keep[o_mine, :] + k.do_y_in[...].astype(f3)
+    k.do_x[...] = k.do_keep[at(y * o_quarter + (1 - x) * o_eighth, o_eighth), :].astype(bf)
+    wires.send(k.do_x, k.do_x_in, in_do + 2, (x_s, v))
     def o_at(q, j):
         at_c, at_x, at_y, at_z = q % 2, q // 2, j % 2, j // 2
         return o_grad.at[at(at_c * o_half + at_y * o_quarter + at_x * o_eighth + at_z * o_piece, o_piece)]
@@ -949,6 +955,31 @@
             wires.send(w_query(j), w_query(j), in_query + j, (s, y_v))
         to_mate(1, w_query(j))
 
+    across = 1 - y
+    pass_plane(z, across)
+
+    load_w.wait()
+    for p in view_peers:
+        wires.wait(k.pc_tok.at[:, :, at(p * own, own)], in_pc + p)
+
+    def back_tile(n, unused):
+        cols = at(n * tile, tile)
+        total = dot_inner(k.pc_tok[0], k.w_full[cols, pl.ds(0, width)])
+        for t in range(1, 3):
+            total = total + dot_inner(k.pc_tok[t], k.w_full[cols, pl.ds(t * width, width)])
+        k.part_own[0, 0, :, cols] = total
+        return unused
+
+    lax.fori_loop(0, width // tile, back_tile, 0)
+    unit_one, inverse_one = norm_stats(tok[...].astype(f3))
+    cot_one = k.part_own[0, 0]
+    k.gain_own[0:1, :] = jnp.sum(cot_one * unit_one, axis=0, keepdims=True)
+    k.gain_own[2:8, :] = jnp.zeros((6, width), f3)
+    tokens_grad[...] = tokens_grad[...] + norm_back(cot_one, unit_one, inverse_one, gain_one)
+    for p in seq_peers:
+        wires.send(k.gain_own, k.gain_in.at[s], in_gain + s, (p, v))
+    kept.append(load(tokens_grad, tokens_hbm))
+
     wires.wait(k.do_x_in, in_do + 2)
     total = k.do_keep[at(y * o_quarter + x * o_eighth, o_eighth), :] + k.do_x_in[...].astype(f3)
     k.do_z[...] = total.astype(bf)
@@ -959,11 +990,19 @@
     for zt in others_z:
         wires.send(k.do_z.at[o_level(zt)], k.do_z_in.at[z], in_do_z + z, level(zt))
 
-    across = 1 - y
-    for zt in others_z:
-        pass_plane(zt, y)
-    for zt in others_z:
-        pass_query(zt, y)
+    pass_plane(z_pair, y)
+    pass_plane(z_two, y)
+    pass_query(z, across)
+    pass_plane(z_pair, across)
+    pass_query(z_pair, y)
+    pass_query(z_two, y)
+    pass_plane(z_flip, y)
+    pass_plane(z_two, across)
+    there = at((y * 2 + 1 - high) * hidden, hidden)
+    k.grad_pass[1, there, :] = grad_block(1, 0, 1 - high).astype(bf)
+    kept.append(load(k.grad_pass.at[1, there], up_away))
+    up_grad[...] = grad_block(1, 1, high)
+    kept.append(load(up_grad, up_part))
     total = k.do_keep[at(y * o_quarter + x * o_eighth + z * o_piece, o_piece), :]
     total = total + k.do_x_in[o_level(z), :].astype(f3)
     for zt in others_z:
@@ -975,10 +1014,9 @@
     wires.send(k.do_own, o_at(s, v), in_out[1] + v, (x_s, v))
     wires.send(k.do_own, o_at(s, v), in_out_mate, (c_s, v), bulk=to_mate_o)
     kept.append(load(k.do_own, o_at(s, v)))
-    send_far(1)
-    for zt in [z] + others_z:
-        pass_plane(zt, across)
-    for zt in [z] + others_z:
+    pass_query(z_flip, y)
+    pass_plane(z_flip, across)
+    for zt in others_z:
         pass_query(zt, across)
 
     total = k.gain_own[...]
@@ -1005,14 +1043,12 @@
 
     for zt in others_z:
         pass_out(zt, y)
-    send_joined(1)
+    grads_to_z(0)
     for zt in [z] + others_z:
         pass_out(zt, across)
 
     layer_out[...] = (k.middle[...] + live * part_sum(1)).astype(bf)
     kept.append(load(layer_out, layer_hbm))
-    collect(0, down_grad)
-    kept.append(load(down_grad, down_hbm_out))
     by_arrival = [v] + [zt * 2 + y for zt in others_z] + [zt * 2 + across for zt in [z] + others_z]
     for j in by_arrival:
         wires.wait(w_cross(x_s, j), in_cross + j)
@@ -1020,8 +1056,6 @@
     for j in by_arrival:
         wires.wait(o_at(x_s, j), in_out[1] + j)
         out_mate(x_s, j)
-    collect(1, up_grad)
-    kept.append(load(up_grad, up_hbm_out))
 
     total = k.gain_sum[...]
     for p in view_peers:
@@ -1029,6 +1063,8 @@
         total = total + k.gain_all[p]
     gains[...] = total
 
+    collect(0, down_grad)
+    kept.append(load(down_grad, down_hbm_out))
     def w_rows(q, first, last):
         return w_grad.at[pl.ds(first, last - first), at(q * part, part)]
 
@@ -1060,12 +1096,12 @@
 
 
 def finish_kernel(*refs):
-    (layer_in, tokens_in, gains, w_in, o_in, up_in, down_in) = refs[:7]
-    (layer_out, tokens_grad, gain_one, w_out, o_out, gain_two, up_out, down_out) = refs[7:15]
-    (layer, tokens, up, down, w_narrow, o_narrow, w_wide, o_wide, in_sem, out_sem) = refs[15:]
+    (layer_in, tokens_in, gains, w_in, o_in, down_in) = refs[:6]
+    (layer_out, tokens_grad, gain_one, w_out, o_out, gain_two, down_out) = refs[6:13]
+    (layer, tokens, down, w_narrow, o_narrow, w_wide, o_wide, in_sem, out_sem) = refs[13:]
     width = o_in.shape[0]
     tall = width // FINISH_STEPS
-    asis = ((layer_in, layer, layer_out), (tokens_in, tokens, tokens_grad), (up_in, up, up_out), (down_in, down, down_out))
+    asis = ((layer_in, layer, layer_out), (tokens_in, tokens, tokens_grad), (down_in, down, down_out))
 
     def rows(i):
         return pl.ds(i * tall, tall)
@@ -1118,7 +1154,7 @@
     anywhere = pl.BlockSpec(memory_space=pl.ANY)
     shape = jax.ShapeDtypeStruct
     bf, f3 = jnp.bfloat16, jnp.float32
-    parts = pl.pallas_call(
+    layer_raw, tokens_raw, gains, w_raw, o_raw, up_part, up_away, down_raw = pl.pallas_call(
         functools.partial(layer_kernel, tuple(spec), seqs, views),
         out_shape=(
             shape((rows, width), bf),
@@ -1127,10 +1163,11 @@
             shape((3, width, width), bf),
             shape((width, width), bf),
             shape((hidden, width), f3),
+            shape((hidden, width), bf),
             shape((hidden, width), f3),
         ),
         in_specs=[anywhere, vmem, vmem, anywhere, vmem, vmem] + [anywhere] * 4,
-        out_specs=(anywhere, anywhere, vmem, anywhere, anywhere, anywhere, anywhere),
+        out_specs=(anywhere, anywhere, vmem) + (anywhere,) * 5,
         scratch_shapes=list(spec.values()),
         compiler_params=pltpu.CompilerParams(
             collective_id=0, has_side_effects=True, vmem_limit_bytes=67043328
@@ -1148,7 +1185,9 @@
         up_weight,
         down_weight,
     )
-    layer_out, tokens_grad, gain_one, w_grad, o_grad, gain_two, up_grad, down_grad = pl.pallas_call(
+    shift = [(j, (j + views // 2) % views) for j in range(views)]
+    up_grad = up_part + lax.ppermute(up_away, "view", shift).astype(f3)
+    layer_out, tokens_grad, gain_one, w_grad, o_grad, gain_two, down_grad = pl.pallas_call(
         finish_kernel,
         out_shape=(
             shape((rows, width), bf),
@@ -1158,14 +1197,12 @@
             shape((width, width), f3),
             shape((width,), f3),
             shape((hidden, width), f3),
-            shape((hidden, width), f3),
         ),
-        in_specs=[anywhere] * 2 + [vmem] + [anywhere] * 4,
-        out_specs=(anywhere, anywhere, vmem, anywhere, anywhere, vmem, anywhere, anywhere),
+        in_specs=[anywhere] * 2 + [vmem] + [anywhere] * 3,
+        out_specs=(anywhere, anywhere, vmem, anywhere, anywhere, vmem, anywhere),
         scratch_shapes=[
             pltpu.VMEM((rows, width), bf),
             pltpu.VMEM((rows, width), f3),
-            pltpu.VMEM((hidden, width), f3),
             pltpu.VMEM((hidden, width), f3),
             pltpu.VMEM((3, width, width), bf),
             pltpu.VMEM((width, width), bf),
@@ -1174,8 +1211,11 @@
             pltpu.SemaphoreType.DMA((2 * FINISH_STEPS + 4,)),
             pltpu.SemaphoreType.DMA((2 * FINISH_STEPS + 4,)),
         ],
+        cost_estimate=pl.CostEstimate(
+            flops=4 * width * width, transcendentals=0, bytes_accessed=28 * width * width
+        ),
         name="finish",
-    )(*parts)
+    )(layer_raw, tokens_raw, gains, w_raw, o_raw, down_raw)
     return (
         layer_out[None],
         tokens_grad[None],

time: 190 us -> 184 us (0.968)
  Pallas kernels: 188 us -> 178 us
  waiting for transfers between devices: 0 us -> 4.12 us
    pallas_call x1, Pallas kernels: 177 us -> 168 us  [fused(): pl.pallas_call(functools.partial(layer_kernel, tuple(spec), seqs, views),...]
    ppermute x0 -> x1, waiting for transfers between devices: none -> 4.12 us  [fused(): up_grad = up_part + lax.ppermute(up_away, 'view', shift).astype(f3)]
  transfers between devices with their start and end apart: 0 -> 1, of which waited for: 0 -> 1; matrix products, arithmetic and copies ran while one was open for 0% -> 0% of each run, Pallas kernels for 0% -> 6%
where the time goes in v4:
time: 184 us
  Pallas kernels  178 us (97%)
  waiting for transfers between devices  4.12 us (2%)
    pallas_call x1, Pallas kernels, fused(): pl.pallas_call(functools.partial(layer_kernel, tuple(spec), seqs, views),...  168 us
    pallas_call x1, Pallas kernels, fused(): pl.pallas_call(finish_kernel, out_shape=(shape((rows, width), bf), shape(...  10.5 us
    ppermute x1, waiting for transfers between devices, fused(): up_grad = up_part + lax.ppermute(up_away, 'view', shift).astype(f3)  4.12 us
  transfers between devices with their start and end apart: 1, of which 1 were waited for; matrix products, arithmetic and copies ran while one was open for 0% of the time, Pallas kernels for 6%

profile of v4, /device:TPU:0, one launch (start us, length us, event | category | flops | bytes accessed | tf_op | source)
XLA Modules:
  0.0 183.9 jit_solution(4824567328128627673)
XLA Ops:
  0.6 167.7 %layer.1 = (bf16[128,1024]{1,0:T(8,128)(2,1)}, f32[128,1024]{1,0:T(8,128)}, f32[8,1024]{1,0:T(8,128)}, bf16[3,1024,1024]{2,1,0:T(8,128)(2,1)}, bf16[1024,1024]{1...) custom-call(bf16[128,1024]{1,0:T(8,128)(2,1)} %bitcast.4, ...), custom_call_target="tpu_custom_call" | custom-call | tf_op jit(solution)/shard_map/layer/pallas_call | solution.py:1157
  168.3 0.0 copy-start
  168.3 0.1 collective-permute-start
  168.4 10.5 %finish.1 = (bf16[128,1024]{1,0:T(8,128)(2,1)}, f32[128,1024]{1,0:T(8,128)}, f32[1024]{0:T(1024)}, f32[1024,3072]{1,0:T(8,128)}, f32[1024,1024]{1,0:T(8,128)}, /*index=5*/f32[1024]{0:T(1024)}, f32[128,1024]{1,0:T(8,128)}) custom-call(bf16[128,1024]{1,0:T(8,128)(2,1)} %get-tuple-element.23.refs_0_, f32[128,1024]{1,0:T(8,128)} %get-tuple-element.24.refs_1_, ...), custom_call_target="tpu_custom_call" | custom-call | flops 4194304 | bytes 29360128 | tf_op jit(solution)/shard_map/finish/pallas_call | solution.py:1190
  178.9 4.1 %collective-permute-done = bf16[128,1024]{1,0:T(8,128)(2,1)S(1)} collective-permute-done((bf16[128,1024]{1,0:T(8,128)(2,1)}, bf16[128,1024]{1,0:T(8,128)(2,1)S(1)}, u32[]{:S(2)}, u32[]{:S(2)}) %collective-permute-start) | collective-permute-done | bytes 262176 | tf_op jit(solution)/shard_map/ppermute | solution.py:1189
  183.1 0.0 copy-done
  183.1 0.8 convert_add_fusion
Async XLA Ops:
  168.3 14.7 %copy-start = (f32[128,1024]{1,0:T(8,128)S(1)}, f32[128,1024]{1,0:T(8,128)}, u32[]{:S(2)}) copy-start(f32[128,1024]{1,0:T(8,128)} %get-tuple-element.35) | copy-start | bytes 1572868
  168.3 14.7 %collective-permute-start = (bf16[128,1024]{1,0:T(8,128)(2,1)}, bf16[128,1024]{1,0:T(8,128)(2,1)S(1)}, u32[]{:S(2)}, u32[]{:S(2)}) collective-permute-start(bf16[128,1024]{1,0:T(8,128)(2,1)} %get-tuple-element.36), channel_id=1, source_target_pairs={{0,4},{1,5},{2,6},{3,7},{4,0},{5,1},{6,2},{7,3},{8,12},{9,13},{10,... | collective-permute-start | bytes 786440 | tf_op jit(solution)/shard_map/ppermute | solution.py:1189

commit v5 on v4

--- a/solution.py
+++ b/solution.py
@@ -382,10 +382,10 @@
         dw_own=vm((3, width // seqs, own), bf),
         do_core=vm((half, width), bf),
         do_core_in=vm((half, width), bf),
-        do_y=vm((quarter, width), bf),
-        do_y_in=vm((quarter, width), bf),
-        do_x=vm((eighth, width), bf),
-        do_x_in=vm((eighth, width), bf),
+        do_first=vm((quarter, width), bf),
+        do_first_in=vm((quarter, width), bf),
+        do_second=vm((eighth, width), bf),
+        do_second_in=vm((eighth, width), bf),
         do_z=vm((eighth, width), bf),
         do_z_in=vm((LEVELS, eighth // LEVELS, width), bf),
         do_own=vm((eighth // LEVELS, width), bf),
@@ -639,7 +639,7 @@
         k.att_s[here, :] = result
         return unused
 
-    lax.fori_loop(0, SLOTS, attend, 0)
+    lax.fori_loop(0, SLOTS, attend, 0, unroll=True)
     reorder(k.att, k.att_s, 8)
     own_cols = at(v * own, own)
     for p in view_peers:
@@ -666,6 +666,8 @@
         square_send(k.normed_two, in_two, own_slot, device)
 
     core_exchange(k.up, in_up)
+    square_relay(k.normed_two, in_two)
+    mlp_relay(k.down, in_down)
     wires.wait(k.up.at[at((1 - c) * half, half)], in_up + LEVELS)
 
     def hidden_tiles(slot):
@@ -682,8 +684,6 @@
         lax.fori_loop(0, mlp_rows // tile, step, 0)
 
     hidden_tiles(own_slot)
-    mlp_relay(k.down, in_down)
-    square_relay(k.normed_two, in_two)
     hidden_tiles(pair_slot)
     for slot in (x_slot, far_slot):
         wires.wait(slot_rows(k.normed_two, slot), in_two + slot)
@@ -784,7 +784,6 @@
     grad_halves(1, k.hid_cot, k.normed_two)
     part_tiles(1, k.act, k.down)
     part_join(0)
-    grads_to_y(1)
 
     def part_sum(which):
         total = k.part_own[which, 0]
@@ -828,11 +827,12 @@
     outer_rows(c * o_half, k.do_keep, f3)
     wires.wait(k.do_core_in, in_do)
     k.do_keep[...] = k.do_keep[...] + k.do_core_in[...].astype(f3)
-    k.do_y[...] = k.do_keep[at((1 - y) * o_quarter, o_quarter), :].astype(bf)
-    wires.send(k.do_y, k.do_y_in, in_do + 1, (s, y_v))
+    k.do_first[...] = k.do_keep[at((1 - x) * o_quarter, o_quarter), :].astype(bf)
+    wires.send(k.do_first, k.do_first_in, in_do + 1, (x_s, v))
 
     for p in view_peers:
         wires.wait(view_rows(k.acot, p), in_acot + p)
+    grads_to_y(1)
     part_join(1)
     reorder(k.acot_s, k.acot, 0)
 
@@ -861,7 +861,7 @@
             k.pc_s[here, pl.ds(t * own, own)] = outs[t].astype(bf)
         return unused
 
-    lax.fori_loop(0, SLOTS, attend_back, 0)
+    lax.fori_loop(0, SLOTS, attend_back, 0, unroll=True)
     pc_blocks = k.pc_s.reshape(count, block, 3 * own)
 
     def unsort(i, unused):
@@ -924,14 +924,14 @@
     z_cast(w_query(v), w_query(v), in_query + v)
     wires.send(w_query(v), w_query(v), in_mate[1], (c_s, v), bulk=to_mate_w[1])
 
-    wires.wait(k.do_y_in, in_do + 1)
-    o_mine = at(y * o_quarter, o_quarter)
-    k.do_keep[o_mine, :] = k.do_keep[o_mine, :] + k.do_y_in[...].astype(f3)
-    k.do_x[...] = k.do_keep[at(y * o_quarter + (1 - x) * o_eighth, o_eighth), :].astype(bf)
-    wires.send(k.do_x, k.do_x_in, in_do + 2, (x_s, v))
+    wires.wait(k.do_first_in, in_do + 1)
+    o_mine = at(x * o_quarter, o_quarter)
+    k.do_keep[o_mine, :] = k.do_keep[o_mine, :] + k.do_first_in[...].astype(f3)
+    k.do_second[...] = k.do_keep[at(x * o_quarter + (1 - y) * o_eighth, o_eighth), :].astype(bf)
+    wires.send(k.do_second, k.do_second_in, in_do + 2, (s, y_v))
     def o_at(q, j):
         at_c, at_x, at_y, at_z = q % 2, q // 2, j % 2, j // 2
-        return o_grad.at[at(at_c * o_half + at_y * o_quarter + at_x * o_eighth + at_z * o_piece, o_piece)]
+        return o_grad.at[at(at_c * o_half + at_x * o_quarter + at_y * o_eighth + at_z * o_piece, o_piece)]
 
     def to_mate(which, ref):
         wires.send(ref, ref, in_mate[which], (c_s, v), bulk=to_mate_w[which])
@@ -980,8 +980,8 @@
         wires.send(k.gain_own, k.gain_in.at[s], in_gain + s, (p, v))
     kept.append(load(tokens_grad, tokens_hbm))
 
-    wires.wait(k.do_x_in, in_do + 2)
-    total = k.do_keep[at(y * o_quarter + x * o_eighth, o_eighth), :] + k.do_x_in[...].astype(f3)
+    wires.wait(k.do_second_in, in_do + 2)
+    total = k.do_keep[at(x * o_quarter + y * o_eighth, o_eighth), :] + k.do_second_in[...].astype(f3)
     k.do_z[...] = total.astype(bf)
 
     def o_level(zt):
@@ -1003,8 +1003,8 @@
     kept.append(load(k.grad_pass.at[1, there], up_away))
     up_grad[...] = grad_block(1, 1, high)
     kept.append(load(up_grad, up_part))
-    total = k.do_keep[at(y * o_quarter + x * o_eighth + z * o_piece, o_piece), :]
-    total = total + k.do_x_in[o_level(z), :].astype(f3)
+    total = k.do_keep[at(x * o_quarter + y * o_eighth + z * o_piece, o_piece), :]
+    total = total + k.do_second_in[o_level(z), :].astype(f3)
     for zt in others_z:
         wires.wait(k.do_z_in.at[zt], in_do_z + zt)
         total = total + k.do_z_in[zt].astype(f3)

time: 184 us -> 180 us (0.978)
  waiting for transfers between devices: 4.12 us -> 0.73 us
  Pallas kernels: 178 us -> 176 us
    ppermute x1, waiting for transfers between devices: 4.12 us -> 0.73 us  [fused(): up_grad = up_part + lax.ppermute(up_away, 'view', shift).astype(f3)]
    pallas_call x1, Pallas kernels: 168 us -> 165 us  [fused(): pl.pallas_call(functools.partial(layer_kernel, tuple(spec), seqs, views),...]
where the time goes in v5:
time: 180 us; the launch traced here: 178 us
  Pallas kernels  176 us (98%)
    pallas_call x1, Pallas kernels, fused(): pl.pallas_call(functools.partial(layer_kernel, tuple(spec), seqs, views),...  165 us
    pallas_call x1, Pallas kernels, fused(): pl.pallas_call(finish_kernel, out_shape=(shape((rows, width), bf), shape(...  10.5 us
  transfers between devices with their start and end apart: 1, of which 1 were waited for; matrix products, arithmetic and copies ran while one was open for 0% of the time, Pallas kernels for 6%

profile of v5, /device:TPU:0, one launch (start us, length us, event | category | flops | bytes accessed | tf_op | source)
XLA Modules:
  0.0 178.2 jit_solution(459912018722226532)
XLA Ops:
  0.6 165.3 %layer.1 = (bf16[128,1024]{1,0:T(8,128)(2,1)}, f32[128,1024]{1,0:T(8,128)}, f32[8,1024]{1,0:T(8,128)}, bf16[3,1024,1024]{2,1,0:T(8,128)(2,1)}, bf16[1024,1024]{1...) custom-call(bf16[128,1024]{1,0:T(8,128)(2,1)} %bitcast.4, ...), custom_call_target="tpu_custom_call" | custom-call | tf_op jit(solution)/shard_map/layer/pallas_call | solution.py:1157
  166.0 0.0 copy-start
  166.0 0.1 collective-permute-start
  166.1 10.5 %finish.1 = (bf16[128,1024]{1,0:T(8,128)(2,1)}, f32[128,1024]{1,0:T(8,128)}, f32[1024]{0:T(1024)}, f32[1024,3072]{1,0:T(8,128)}, f32[1024,1024]{1,0:T(8,128)}, /*index=5*/f32[1024]{0:T(1024)}, f32[128,1024]{1,0:T(8,128)}) custom-call(bf16[128,1024]{1,0:T(8,128)(2,1)} %get-tuple-element.23.refs_0_, f32[128,1024]{1,0:T(8,128)} %get-tuple-element.24.refs_1_, ...), custom_call_target="tpu_custom_call" | custom-call | flops 4194304 | bytes 29360128 | tf_op jit(solution)/shard_map/finish/pallas_call | solution.py:1190
  176.6 0.7 collective-permute-done
  177.3 0.0 copy-done
  177.3 0.8 convert_add_fusion
Async XLA Ops:
  166.0 11.3 %copy-start = (f32[128,1024]{1,0:T(8,128)S(1)}, f32[128,1024]{1,0:T(8,128)}, u32[]{:S(2)}) copy-start(f32[128,1024]{1,0:T(8,128)} %get-tuple-element.35) | copy-start | bytes 1572868
  166.0 11.3 %collective-permute-start = (bf16[128,1024]{1,0:T(8,128)(2,1)}, bf16[128,1024]{1,0:T(8,128)(2,1)S(1)}, u32[]{:S(2)}, u32[]{:S(2)}) collective-permute-start(bf16[128,1024]{1,0:T(8,128)(2,1)} %get-tuple-element.36), channel_id=1, source_target_pairs={{0,4},{1,5},{2,6},{3,7},{4,0},{5,1},{6,2},{7,3},{8,12},{9,13},{10,... | collective-permute-start | bytes 786440 | tf_op jit(solution)/shard_map/ppermute | solution.py:1189

commit v6 on v5

--- a/solution.py
+++ b/solution.py
@@ -320,7 +320,7 @@
         self.copy(dst, dst, 0, slot, self.peer).wait_recv()
 
 
-SENDS, RECVS, LOCALS = 88, 136, 20
+SENDS, RECVS, LOCALS = 67, 126, 17
 LEVELS = 4
 
 
@@ -828,7 +828,6 @@
     wires.wait(k.do_core_in, in_do)
     k.do_keep[...] = k.do_keep[...] + k.do_core_in[...].astype(f3)
     k.do_first[...] = k.do_keep[at((1 - x) * o_quarter, o_quarter), :].astype(bf)
-    wires.send(k.do_first, k.do_first_in, in_do + 1, (x_s, v))
 
     for p in view_peers:
         wires.wait(view_rows(k.acot, p), in_acot + p)
@@ -913,6 +912,7 @@
         return w_at(q, j, 1, 3)
 
     wires.send(k.dw_own.at[pl.ds(0, 1)], w_at(s, v, 0, 1), in_query + v, (x_s, v))
+    wires.send(k.do_first, k.do_first_in, in_do + 1, (x_s, v))
     wires.send(k.dw_own, w_plane(v), in_plane + v, (s, y_v))
     z_cast(k.dw_own, w_plane(v), in_plane + v)
     wires.send(k.dw_own.at[pl.ds(1, 2)], w_cross(s, v), in_cross + v, (x_s, v))

time: 180 us -> 177 us (0.983)
  Pallas kernels: 176 us -> 174 us
    pallas_call x1, Pallas kernels: 165 us -> 163 us  [fused(): pl.pallas_call(functools.partial(layer_kernel, tuple(spec), seqs, views),...]
where the time goes in v6:
time: 177 us
  Pallas kernels  174 us (98%)
    pallas_call x1, Pallas kernels, fused(): pl.pallas_call(functools.partial(layer_kernel, tuple(spec), seqs, views),...  163 us
    pallas_call x1, Pallas kernels, fused(): pl.pallas_call(finish_kernel, out_shape=(shape((rows, width), bf), shape(...  10.5 us
  transfers between devices with their start and end apart: 1, of which 1 were waited for; matrix products, arithmetic and copies ran while one was open for 0% of the time, Pallas kernels for 6%

profile of v6, /device:TPU:0, one launch (start us, length us, event | category | flops | bytes accessed | tf_op | source)
XLA Modules:
  0.0 176.7 jit_solution(5617485429406416243)
XLA Ops:
  0.6 163.1 %layer.1 = (bf16[128,1024]{1,0:T(8,128)(2,1)}, f32[128,1024]{1,0:T(8,128)}, f32[8,1024]{1,0:T(8,128)}, bf16[3,1024,1024]{2,1,0:T(8,128)(2,1)}, bf16[1024,1024]{1...) custom-call(bf16[128,1024]{1,0:T(8,128)(2,1)} %bitcast.4, ...), custom_call_target="tpu_custom_call" | custom-call | tf_op jit(solution)/shard_map/layer/pallas_call | solution.py:1157
  163.7 0.0 copy-start
  163.7 0.1 collective-permute-start
  163.8 10.5 %finish.1 = (bf16[128,1024]{1,0:T(8,128)(2,1)}, f32[128,1024]{1,0:T(8,128)}, f32[1024]{0:T(1024)}, f32[1024,3072]{1,0:T(8,128)}, f32[1024,1024]{1,0:T(8,128)}, /*index=5*/f32[1024]{0:T(1024)}, f32[128,1024]{1,0:T(8,128)}) custom-call(bf16[128,1024]{1,0:T(8,128)(2,1)} %get-tuple-element.23.refs_0_, f32[128,1024]{1,0:T(8,128)} %get-tuple-element.24.refs_1_, ...), custom_call_target="tpu_custom_call" | custom-call | flops 4194304 | bytes 29360128 | tf_op jit(solution)/shard_map/finish/pallas_call | solution.py:1190
  174.3 1.5 collective-permute-done
  175.8 0.0 copy-done
  175.8 0.8 convert_add_fusion
Async XLA Ops:
  163.7 12.1 %copy-start = (f32[128,1024]{1,0:T(8,128)S(1)}, f32[128,1024]{1,0:T(8,128)}, u32[]{:S(2)}) copy-start(f32[128,1024]{1,0:T(8,128)} %get-tuple-element.35) | copy-start | bytes 1572868
  163.7 12.1 %collective-permute-start = (bf16[128,1024]{1,0:T(8,128)(2,1)}, bf16[128,1024]{1,0:T(8,128)(2,1)S(1)}, u32[]{:S(2)}, u32[]{:S(2)}) collective-permute-start(bf16[128,1024]{1,0:T(8,128)(2,1)} %get-tuple-element.36), channel_id=1, source_target_pairs={{0,4},{1,5},{2,6},{3,7},{4,0},{5,1},{6,2},{7,3},{8,12},{9,13},{10,... | collective-permute-start | bytes 786440 | tf_op jit(solution)/shard_map/ppermute | solution.py:1189

commit v7 on v6

--- a/solution.py
+++ b/solution.py
@@ -618,7 +618,7 @@
             dst[at(i * block, block), :] = blocks[from_block].astype(dst.dtype)
             return unused
 
-        lax.fori_loop(0, count, step, 0, unroll=8)
+        lax.fori_loop(0, count, step, 0, unroll=16)
 
     reorder(k.qkv_s, k.qkv, 0)
 
@@ -829,10 +829,10 @@
     k.do_keep[...] = k.do_keep[...] + k.do_core_in[...].astype(f3)
     k.do_first[...] = k.do_keep[at((1 - x) * o_quarter, o_quarter), :].astype(bf)
 
+    grads_to_y(1)
+    part_join(1)
     for p in view_peers:
         wires.wait(view_rows(k.acot, p), in_acot + p)
-    grads_to_y(1)
-    part_join(1)
     reorder(k.acot_s, k.acot, 0)
 
     def attend_back(g, unused):
@@ -870,7 +870,7 @@
             k.pc[t, at(i * block, block), :] = found[:, t * own : (t + 1) * own]
         return unused
 
-    lax.fori_loop(0, count, unsort, 0, unroll=8)
+    lax.fori_loop(0, count, unsort, 0, unroll=16)
     for p in view_peers:
         wires.send(k.pc.at[:, at(p * rows, rows)], k.pc_tok.at[:, :, own_cols], in_pc + v, (s, p), bulk=to_view[3])
     for t in range(3):

time: 177 us -> 176 us (level)
  no operation moved by 1% of the time
where the time goes in v7:
time: 176 us
  Pallas kernels  173 us (98%)
    pallas_call x1, Pallas kernels, fused(): pl.pallas_call(functools.partial(layer_kernel, tuple(spec), seqs, views),...  163 us
    pallas_call x1, Pallas kernels, fused(): pl.pallas_call(finish_kernel, out_shape=(shape((rows, width), bf), shape(...  10.5 us
  transfers between devices with their start and end apart: 1, of which 1 were waited for; matrix products, arithmetic and copies ran while one was open for 0% of the time, Pallas kernels for 6%

profile of v7, /device:TPU:0, one launch (start us, length us, event | category | flops | bytes accessed | tf_op | source)
XLA Modules:
  0.0 176.2 jit_solution(3166320295155402125)
XLA Ops:
  0.6 162.9 %layer.1 = (bf16[128,1024]{1,0:T(8,128)(2,1)}, f32[128,1024]{1,0:T(8,128)}, f32[8,1024]{1,0:T(8,128)}, bf16[3,1024,1024]{2,1,0:T(8,128)(2,1)}, bf16[1024,1024]{1...) custom-call(bf16[128,1024]{1,0:T(8,128)(2,1)} %bitcast.4, ...), custom_call_target="tpu_custom_call" | custom-call | tf_op jit(solution)/shard_map/layer/pallas_call | solution.py:1157
  163.5 0.0 copy-start
  163.5 0.1 collective-permute-start
  163.6 10.5 %finish.1 = (bf16[128,1024]{1,0:T(8,128)(2,1)}, f32[128,1024]{1,0:T(8,128)}, f32[1024]{0:T(1024)}, f32[1024,3072]{1,0:T(8,128)}, f32[1024,1024]{1,0:T(8,128)}, /*index=5*/f32[1024]{0:T(1024)}, f32[128,1024]{1,0:T(8,128)}) custom-call(bf16[128,1024]{1,0:T(8,128)(2,1)} %get-tuple-element.23.refs_0_, f32[128,1024]{1,0:T(8,128)} %get-tuple-element.24.refs_1_, ...), custom_call_target="tpu_custom_call" | custom-call | flops 4194304 | bytes 29360128 | tf_op jit(solution)/shard_map/finish/pallas_call | solution.py:1190
  174.1 1.2 collective-permute-done
  175.3 0.0 copy-done
  175.4 0.8 convert_add_fusion
Async XLA Ops:
  163.5 11.9 %copy-start = (f32[128,1024]{1,0:T(8,128)S(1)}, f32[128,1024]{1,0:T(8,128)}, u32[]{:S(2)}) copy-start(f32[128,1024]{1,0:T(8,128)} %get-tuple-element.35) | copy-start | bytes 1572868
  163.5 11.8 %collective-permute-start = (bf16[128,1024]{1,0:T(8,128)(2,1)}, bf16[128,1024]{1,0:T(8,128)(2,1)S(1)}, u32[]{:S(2)}, u32[]{:S(2)}) collective-permute-start(bf16[128,1024]{1,0:T(8,128)(2,1)} %get-tuple-element.36), channel_id=1, source_target_pairs={{0,4},{1,5},{2,6},{3,7},{4,0},{5,1},{6,2},{7,3},{8,12},{9,13},{10,... | collective-permute-start | bytes 786440 | tf_op jit(solution)/shard_map/ppermute | solution.py:1189

commit v8 on v7

--- a/solution.py
+++ b/solution.py
@@ -745,7 +745,7 @@
         k.hid_cot[:, cols] = (up_to * k.slope[:, cols]).astype(bf)
         return unused
 
-    lax.fori_loop(0, mlp_rows // tile, cot_tile, 0)
+    lax.fori_loop(0, mlp_rows // tile, cot_tile, 0, unroll=True)
 
     strip = width // 2
 
@@ -760,7 +760,7 @@
                 k.part_all[:, cols] = dot_nn(left[...], right[:, cols])
                 return unused
 
-            lax.fori_loop(0, strip // tile, step, 0)
+            lax.fori_loop(0, strip // tile, step, 0, unroll=True)
             cols = strip_cols(i)
             k.part_out[which, 0, :, cols] = k.part_all[at(far_slot * rows, rows), cols].astype(bf)
             there = k.part_out.at[which, 0, :, cols], k.part_in.at[which, 0, :, cols]

time: 176 us -> 177 us (level)
  no operation moved by 1% of the time
where the time goes in v8:
time: 177 us
  Pallas kernels  173 us (98%)
  waiting for transfers between devices  2.48 us (1%)
    pallas_call x1, Pallas kernels, fused(): pl.pallas_call(functools.partial(layer_kernel, tuple(spec), seqs, views),...  162 us
    pallas_call x1, Pallas kernels, fused(): pl.pallas_call(finish_kernel, out_shape=(shape((rows, width), bf), shape(...  10.5 us
  transfers between devices with their start and end apart: 1, of which 1 were waited for; matrix products, arithmetic and copies ran while one was open for 0% of the time, Pallas kernels for 6%

profile of v8, /device:TPU:0, one launch (start us, length us, event | category | flops | bytes accessed | tf_op | source)
XLA Modules:
  0.0 177.0 jit_solution(13527945611077894218)
XLA Ops:
  0.6 162.4 %layer.1 = (bf16[128,1024]{1,0:T(8,128)(2,1)}, f32[128,1024]{1,0:T(8,128)}, f32[8,1024]{1,0:T(8,128)}, bf16[3,1024,1024]{2,1,0:T(8,128)(2,1)}, bf16[1024,1024]{1...) custom-call(bf16[128,1024]{1,0:T(8,128)(2,1)} %bitcast.4, ...), custom_call_target="tpu_custom_call" | custom-call | tf_op jit(solution)/shard_map/layer/pallas_call | solution.py:1157
  163.1 0.0 copy-start
  163.1 0.1 collective-permute-start
  163.2 10.5 %finish.1 = (bf16[128,1024]{1,0:T(8,128)(2,1)}, f32[128,1024]{1,0:T(8,128)}, f32[1024]{0:T(1024)}, f32[1024,3072]{1,0:T(8,128)}, f32[1024,1024]{1,0:T(8,128)}, /*index=5*/f32[1024]{0:T(1024)}, f32[128,1024]{1,0:T(8,128)}) custom-call(bf16[128,1024]{1,0:T(8,128)(2,1)} %get-tuple-element.23.refs_0_, f32[128,1024]{1,0:T(8,128)} %get-tuple-element.24.refs_1_, ...), custom_call_target="tpu_custom_call" | custom-call | flops 4194304 | bytes 29360128 | tf_op jit(solution)/shard_map/finish/pallas_call | solution.py:1190
  173.7 2.5 %collective-permute-done = bf16[128,1024]{1,0:T(8,128)(2,1)S(1)} collective-permute-done((bf16[128,1024]{1,0:T(8,128)(2,1)}, bf16[128,1024]{1,0:T(8,128)(2,1)S(1)}, u32[]{:S(2)}, u32[]{:S(2)}) %collective-permute-start) | collective-permute-done | bytes 262176 | tf_op jit(solution)/shard_map/ppermute | solution.py:1189
  176.2 0.0 copy-done
  176.2 0.8 convert_add_fusion
Async XLA Ops:
  163.1 13.1 %copy-start = (f32[128,1024]{1,0:T(8,128)S(1)}, f32[128,1024]{1,0:T(8,128)}, u32[]{:S(2)}) copy-start(f32[128,1024]{1,0:T(8,128)} %get-tuple-element.35) | copy-start | bytes 1572868
  163.1 13.1 %collective-permute-start = (bf16[128,1024]{1,0:T(8,128)(2,1)}, bf16[128,1024]{1,0:T(8,128)(2,1)S(1)}, u32[]{:S(2)}, u32[]{:S(2)}) collective-permute-start(bf16[128,1024]{1,0:T(8,128)(2,1)} %get-tuple-element.36), channel_id=1, source_target_pairs={{0,4},{1,5},{2,6},{3,7},{4,0},{5,1},{6,2},{7,3},{8,12},{9,13},{10,... | collective-permute-start | bytes 786440 | tf_op jit(solution)/shard_map/ppermute | solution.py:1189
